TPU v7x, 32 devices: a whole 2x2x4 slice. The times are simulated.
32 devices in a mesh: parts: 2 (over x), chain: 4 (over z), tile: 4 (over y, core).
Axes of the slice: x: 2, y: 2, z: 4, core: 2. Of those that a mesh axis runs over, the one named last changes fastest.
Arguments:
- leaf_rhs: float32 [8, 64, 128, 512], P(('parts', 'chain'), 'tile'), parts along dimension 0, may hold values from -6 to 6
- leaf_inverse: float32 [8, 64, 128, 128], P(('parts', 'chain'), 'tile'), parts along dimension 0, may hold values from -1 to 2, as said below
- leaf_coupling: float32 [8, 64, 128, 128], P(('parts', 'chain'), 'tile'), parts along dimension 0, may hold values from -0.5 to 0.5
- leaf_update: float32 [8, 64, 128, 128], P(('parts', 'chain'), 'tile'), parts along dimension 0, may hold values from -0.0625 to 0.0625
- update_pattern: int32 [8, 64], P(('parts', 'chain'), 'tile'), parts along dimension 0, may hold values 0 or 1
- sep_rhs: float32 [8, 128, 512], P(('parts', 'chain')), parts along dimension 0, may hold values from -6 to 6
- sep_inverse: float32 [8, 128, 128], P(('parts', 'chain')), parts along dimension 0, may hold values from -1 to 2, as said below
- sep_coupling: float32 [8, 128, 128], P(('parts', 'chain')), parts along dimension 0, may hold values from -0.5 to 0.5
Outputs:
- leaf_solution: float32 [8, 64, 128, 512], P(('parts', 'chain'), 'tile'), parts along dimension 0
- sep_solution: float32 [8, 128, 512], P(('parts', 'chain'), None, 'tile'), parts along dimension 0
There are 2 independent parts, one for each index of `parts`. A program takes and returns all parts, laid end to end along the dimension named above; each array names one. Nothing has to cross between parts.
Inputs may be any that keep to these rules, and one draw needn't show every extreme that they name: `leaf_inverse`: each tile is lower triangular with a diagonal between 0.3 and 2. `sep_inverse`: each tile is lower triangular with a positive diagonal.
All inputs are finite; a program needn't handle non-finite values. No bound on the sum of `update_pattern` on one device may be relied on, other than what follows from the above.
Results may differ from a plain program's by a relative error of at most 0.00017.
Values sent between devices are 32-bit elements; how exact they have to be, the bound alone decides.
No kernel may reach another device: no remote copies, remote signals or barrier semaphores. Data moves between devices by JAX's collectives and lax.ppermute only.
A program may use at most 64 MiB of HBM per device.

v0:
```python
import jax
import jax.numpy as jnp
from jax import lax
from jax.sharding import PartitionSpec as P


def passed_along(block, axis, distance):
    devices = range(lax.axis_size(axis))
    route = [(i - distance, i) for i in devices if i - distance in devices]
    return lax.ppermute(block, axis, route)


def shards(
    leaf_rhs,
    leaf_inverse,
    leaf_coupling,
    leaf_update,
    update_pattern,
    sep_rhs,
    sep_inverse,
    sep_coupling,
):
    highest = lax.Precision.HIGHEST
    inverse_tiles = leaf_inverse[0]
    solved_free = jnp.einsum("lij,ljr->lir", inverse_tiles, leaf_rhs[0], precision=highest)
    gain_tiles = jnp.einsum("lij,ljk->lik", inverse_tiles, leaf_coupling[0], precision=highest)
    masked_update = leaf_update[0] * update_pattern[0].astype(jnp.float32)[:, None, None]
    local_sum = jnp.einsum("lij,ljr->ir", masked_update, solved_free, precision=highest)
    local_cross = jnp.einsum("lij,ljk->ik", masked_update, gain_tiles, precision=highest)
    sep_inv = sep_inverse[0]
    sep_right = sep_rhs[0]
    tile_count = lax.axis_size("tile")
    column_width = sep_right.shape[1] // tile_count
    first_column = lax.axis_index("tile") * column_width
    total_sum, total_cross = lax.psum((local_sum, local_cross), "tile")
    offset = jnp.dot(sep_inv, sep_right - total_sum, precision=highest)
    step_map = -jnp.dot(sep_inv, sep_coupling[0] - total_cross, precision=highest)
    carry_in = jnp.zeros_like(offset)
    for section_turn in range(lax.axis_size("chain") - 1):
        moving = jnp.dot(step_map, carry_in, precision=highest) + offset
        carry_in = passed_along(moving, "chain", 1)
    sep_values = jnp.dot(step_map, carry_in, precision=highest) + offset
    sep_share = lax.dynamic_slice_in_dim(sep_values, first_column, column_width, 1)
    leaf_values = solved_free - jnp.einsum("lik,kr->lir", gain_tiles, carry_in, precision=highest)
    return (leaf_values[None], sep_share[None])


def solution(mesh):
    return jax.shard_map(
        shards,
        mesh=mesh,
        in_specs=(
            P(("parts", "chain"), "tile", None, None),
            P(("parts", "chain"), "tile", None, None),
            P(("parts", "chain"), "tile", None, None),
            P(("parts", "chain"), "tile", None, None),
            P(("parts", "chain"), "tile"),
            P(("parts", "chain"), None, None),
            P(("parts", "chain"), None, None),
            P(("parts", "chain"), None, None),
        ),
        out_specs=(P(("parts", "chain"), "tile", None, None), P(("parts", "chain"), None, "tile")),
        check_vma=False,
    )
```

profile of v0, /device:TPU:0, one launch (start us, length us, event | category | flops | bytes accessed | tf_op | source)
XLA Modules:
  0.0 98.3 jit_solution(9822910758359403547)
XLA Ops:
  7.2 0.0 copy-start
  7.2 0.0 all-reduce.3.cloned.1.call-start
  7.2 0.7 convert_bitcast_fusion
  8.0 0.4 copy-done
  8.4 5.5 %fusion = f32[16,128,512]{2,1,0:T(8,128)S(1)} fusion(f32[1,16,128,512]{3,2,1,0:T(8,128)} %param.8, f32[1,16,128,128]{3,2,1,0:T(8,128)S(1)} %copy-done), kind=kOutput, calls=%fused_computation | convolution fusion | flops 1610612736 | bytes 9437184 | tf_op jit(solution)/shard_map/lij,ljr->lir/dot_general | solution.py:25
  13.9 1.2 %fusion.2 = f32[16,128,128]{2,1,0:T(8,128)S(1)} fusion(f32[1,16,128,128]{3,2,1,0:T(8,128)S(1)} %copy-done.3, f32[1,16,128,128]{3,2,1,0:T(8,128)S(1)} %copy-done), kind=kOutput, calls=%fused_computation.11 | convolution fusion | flops 402653184 | bytes 3145728 | tf_op jit(solution)/shard_map/lij,ljk->lik/dot_general | solution.py:26
  15.2 3.2 %convolution_bitcast_fusion = f32[128,512]{1,0:T(8,128)} fusion(f32[16,128,512]{2,1,0:T(8,128)S(1)} %fusion, f32[1,16,128,128]{3,2,1,0:T(8,128)S(1)} %copy-done.2, f32[16]{0:T(128)S(1)} %convert_bitcast_fusion), kind=kOutput, calls=%fused_computation.5 | convolution fusion | flops 1610874880 | bytes 5505088 | tf_op jit(solution)/shard_map/lij,ljr->ir/dot_general | solution.py:28
  18.4 1.8 %convolution_bitcast_fusion.2 = f32[128,128]{1,0:T(8,128)} fusion(f32[16,128,128]{2,1,0:T(8,128)S(1)} %fusion.2, f32[1,16,128,128]{3,2,1,0:T(8,128)S(1)} %copy-done.2, f32[16]{0:T(128)S(1)} %convert_bitcast_fusion), kind=kOutput, calls=%fused_computation.9 | convolution fusion | flops 402915328 | bytes 2162752 | tf_op jit(solution)/shard_map/lij,ljk->ik/dot_general | solution.py:29
  20.2 0.0 all-reduce.3.cloned.1.call-update
  20.2 35.3 %all-reduce.3.cloned.1.call-done = (f32[128,512]{1,0:T(8,128)}, f32[128,128]{1,0:T(8,128)}) async-done(((f32[128,512]{1,0:T(8,128)}, f32[128,128]{1,0:T(8,128)}), (f32[128,512]{1,0:T(8,128)}, f32[128,128]{1,0:T(8,128)})) %all-reduce.3.cloned.1.call-update) | async-done | bytes 327696 | tf_op jit(solution)/shard_map/psum | solution.py:35
  55.6 1.5 %convolution_bitcast_fusion.1 = f32[128,512]{0,1:T(8,128)S(1)} fusion(f32[128,512]{1,0:T(8,128)} %get-tuple-element.2, f32[1,128,512]{2,1,0:T(8,128)S(1)} %copy-done.4, f32[1,128,128]{2,1,0:T(8,128)S(1)} %copy-done.5), kind=kOutput, calls=%fused_computation.7 | convolution fusion | flops 100728832 | bytes 851968 | tf_op jit(solution)/shard_map/dot_general | solution.py:36
  57.1 1.1 %convolution_negate_fusion = f32[128,128]{1,0:T(8,128)S(1)} fusion(f32[1,128,128]{2,1,0:T(8,128)S(1)} %copy-done.5, f32[128,128]{1,0:T(8,128)} %get-tuple-element.3, f32[1,128,128]{2,1,0:T(8,128)S(1)} %copy-done.6), kind=kOutput, calls=%fused_computation.8 | convolution fusion | flops 25198592 | bytes 262144 | tf_op jit(solution)/shard_map/dot_general | solution.py:37
  58.3 0.4 convolution_add_fusion.2
  58.6 3.4 %collective-permute-start = (f32[128,512]{0,1:T(8,128)S(1)}, f32[128,512]{0,1:T(8,128)S(1)}, u32[]{:S(2)}, u32[]{:S(2)}) collective-permute-start(f32[128,512]{0,1:T(8,128)S(1)} %convolution_add_fusion.2), channel_id=1, source_target_pairs={{0,4},{4,8},{8,12},{1,5},{5,9},{9,13},{2,6},{6,10},{10,14},{3,7},{... | collective-permute-start | bytes 786440 | tf_op jit(solution)/shard_map/ppermute | solution.py:10
  62.1 4.5 %collective-permute-done = f32[128,512]{0,1:T(8,128)S(1)} collective-permute-done((f32[128,512]{0,1:T(8,128)S(1)}, f32[128,512]{0,1:T(8,128)S(1)}, u32[]{:S(2)}, u32[]{:S(2)}) %collective-permute-start) | collective-permute-done | bytes 262176 | tf_op jit(solution)/shard_map/ppermute | solution.py:10
  66.5 0.4 convolution_add_fusion.1
  66.9 4.4 %collective-permute-start.1 = (f32[128,512]{0,1:T(8,128)S(1)}, f32[128,512]{0,1:T(8,128)S(1)}, u32[]{:S(2)}, u32[]{:S(2)}) collective-permute-start(f32[128,512]{0,1:T(8,128)S(1)} %convolution_add_fusion.1), channel_id=1, source_target_pairs={{0,4},{4,8},{8,12},{1,5},{5,9},{9,13},{2,6},{6,10},{10,14},{3,7},{... | collective-permute-start | bytes 786440 | tf_op jit(solution)/shard_map/ppermute | solution.py:10
  71.3 3.9 %collective-permute-done.1 = f32[128,512]{0,1:T(8,128)S(1)} collective-permute-done((f32[128,512]{0,1:T(8,128)S(1)}, f32[128,512]{0,1:T(8,128)S(1)}, u32[]{:S(2)}, u32[]{:S(2)}) %collective-permute-start.1) | collective-permute-done | bytes 262176 | tf_op jit(solution)/shard_map/ppermute | solution.py:10
  75.2 0.4 convolution_add_fusion
  75.5 4.4 %collective-permute-start.2 = (f32[128,512]{0,1:T(8,128)S(1)}, f32[128,512]{0,1:T(8,128)S(1)}, u32[]{:S(2)}, u32[]{:S(2)}) collective-permute-start(f32[128,512]{0,1:T(8,128)S(1)} %convolution_add_fusion), channel_id=1, source_target_pairs={{0,4},{4,8},{8,12},{1,5},{5,9},{9,13},{2,6},{6,10},{10,14},{3,7},{... | collective-permute-start | bytes 786440 | tf_op jit(solution)/shard_map/ppermute | solution.py:10
  79.9 3.9 %collective-permute-done.2 = f32[128,512]{0,1:T(8,128)S(1)} collective-permute-done((f32[128,512]{0,1:T(8,128)S(1)}, f32[128,512]{0,1:T(8,128)S(1)}, u32[]{:S(2)}, u32[]{:S(2)}) %collective-permute-start.2) | collective-permute-done | bytes 262176 | tf_op jit(solution)/shard_map/ppermute | solution.py:10
  83.8 0.4 fusion.13
  84.2 0.7 copy.16
  84.9 6.5 %subtract_bitcast_fusion = f32[1,16,128,512]{3,2,1,0:T(8,128)} fusion(f32[16,128,512]{2,1,0:T(8,128)} %copy-done.1, f32[16,128,128]{2,1,0:T(8,128)S(1)} %fusion.2, f32[128,512]{0,1:T(8,128)S(1)} %collective-permute-done.2), kind=kOutput, calls=%fused_computation.2 | convolution fusion | flops 1611661312 | bytes 9699328 | tf_op jit(solution)/shard_map/lik,kr->lir/dot_general | solution.py:44
  (13 shorter events, 0.1 us)
Async XLA Ops:
  7.2 1.2 %copy-start = (f32[1,16,128,128]{3,2,1,0:T(8,128)S(1)}, f32[1,16,128,128]{3,2,1,0:T(8,128)}, u32[]{:S(2)}) copy-start(f32[1,16,128,128]{3,2,1,0:T(8,128)} %param.9) | copy-start | bytes 3145732
  7.2 48.4 %all-reduce.3.cloned.1.call-start = ((), (), s32[]{:S(2)}) async-start(), calls=%async_computation | async-start | bytes 655360 | tf_op jit(solution)/shard_map/psum | solution.py:35
  8.4 5.5 %copy-start.3 = (f32[1,16,128,128]{3,2,1,0:T(8,128)S(1)}, f32[1,16,128,128]{3,2,1,0:T(8,128)}, u32[]{:S(2)}) copy-start(f32[1,16,128,128]{3,2,1,0:T(8,128)} %param.10) | copy-start | bytes 3145732
  8.4 6.7 %copy-start.2 = (f32[1,16,128,128]{3,2,1,0:T(8,128)S(1)}, f32[1,16,128,128]{3,2,1,0:T(8,128)}, u32[]{:S(2)}) copy-start(f32[1,16,128,128]{3,2,1,0:T(8,128)} %param.11) | copy-start | bytes 3145732
  13.9 4.5 %copy-start.1 = (f32[16,128,512]{2,1,0:T(8,128)}, f32[16,128,512]{2,1,0:T(8,128)S(1)}, u32[]{:S(2)}) copy-start(f32[16,128,512]{2,1,0:T(8,128)S(1)} %fusion) | copy-start | bytes 12582916
  15.1 40.4 %copy-start.4 = (f32[1,128,512]{2,1,0:T(8,128)S(1)}, f32[1,128,512]{2,1,0:T(8,128)}, u32[]{:S(2)}) copy-start(f32[1,128,512]{2,1,0:T(8,128)} %param.13) | copy-start | bytes 786436
  15.1 40.4 %copy-start.5 = (f32[1,128,128]{2,1,0:T(8,128)S(1)}, f32[1,128,128]{2,1,0:T(8,128)}, u32[]{:S(2)}) copy-start(f32[1,128,128]{2,1,0:T(8,128)} %param.14) | copy-start | bytes 196612
  15.2 42.0 %copy-start.6 = (f32[1,128,128]{2,1,0:T(8,128)S(1)}, f32[1,128,128]{2,1,0:T(8,128)}, u32[]{:S(2)}) copy-start(f32[1,128,128]{2,1,0:T(8,128)} %param.15) | copy-start | bytes 196612
  58.6 7.9 %collective-permute-start = (f32[128,512]{0,1:T(8,128)S(1)}, f32[128,512]{0,1:T(8,128)S(1)}, u32[]{:S(2)}, u32[]{:S(2)}) collective-permute-start(f32[128,512]{0,1:T(8,128)S(1)} %convolution_add_fusion.2), channel_id=1, source_target_pairs={{0,4},{4,8},{8,12},{1,5},{5,9},{9,13},{2,6},{6,10},{10,14},{3,7},{... | collective-permute-start | bytes 786440 | tf_op jit(solution)/shard_map/ppermute | solution.py:10
  66.9 8.3 %collective-permute-start.1 = (f32[128,512]{0,1:T(8,128)S(1)}, f32[128,512]{0,1:T(8,128)S(1)}, u32[]{:S(2)}, u32[]{:S(2)}) collective-permute-start(f32[128,512]{0,1:T(8,128)S(1)} %convolution_add_fusion.1), channel_id=1, source_target_pairs={{0,4},{4,8},{8,12},{1,5},{5,9},{9,13},{2,6},{6,10},{10,14},{3,7},{... | collective-permute-start | bytes 786440 | tf_op jit(solution)/shard_map/ppermute | solution.py:10
  75.5 8.3 %collective-permute-start.2 = (f32[128,512]{0,1:T(8,128)S(1)}, f32[128,512]{0,1:T(8,128)S(1)}, u32[]{:S(2)}, u32[]{:S(2)}) collective-permute-start(f32[128,512]{0,1:T(8,128)S(1)} %convolution_add_fusion), channel_id=1, source_target_pairs={{0,4},{4,8},{8,12},{1,5},{5,9},{9,13},{2,6},{6,10},{10,14},{3,7},{... | collective-permute-start | bytes 786440 | tf_op jit(solution)/shard_map/ppermute | solution.py:10
Sparse Core Ops, SparseCore 0:
  20.3 35.1 all-reduce.2
where the time goes:
time: 98.6 us; the launch traced here: 98.3 us
  waiting for transfers between devices  47.5 us (48%)
  matrix products  22.3 us (23%)
  between operations  14.2 us (14%)
  starting transfers between devices  12.2 us (12%)
  local copies, waits for them, and re-layouts  1.22 us (1%)
    psum x1, waiting for transfers between devices, shards(): total_sum, total_cross = lax.psum((local_sum, local_cross), 'tile')  35.3 us
    ppermute x3, starting transfers between devices, passed_along(): return lax.ppermute(block, axis, route)  12.2 us
    ppermute x3, waiting for transfers between devices, passed_along(): return lax.ppermute(block, axis, route)  12.2 us
    dot_general x1, matrix products, shards(): jnp.einsum('lik,kr->lir', gain_tiles, carry_in, precision=highest)  6.52 us
    dot_general x1, matrix products, shards(): jnp.einsum('lij,ljr->lir', inverse_tiles, leaf_rhs[0], precision=highest)  5.46 us
    dot_general x1, matrix products, shards(): jnp.einsum('lij,ljr->ir', masked_update, solved_free, precision=highest)  3.19 us
  transfers between devices with their start and end apart: 4, of which 4 were waited for; matrix products, arithmetic and copies ran while one was open for 0% of the time, Pallas kernels for 0%

commit v1 on v0

v1 whole, which is shorter than its diff:
```python
import jax
import jax.numpy as jnp
from jax import lax
from jax.sharding import PartitionSpec as P

PRECISION = lax.Precision.HIGH


def swapped(block, axis, bit):
    route = [(i, i ^ bit) for i in range(lax.axis_size(axis))]
    return lax.ppermute(block, axis, route)


def product(left, right):
    return jnp.dot(left, right, precision=PRECISION)


def shards(
    leaf_rhs,
    leaf_inverse,
    leaf_coupling,
    leaf_update,
    update_pattern,
    sep_rhs,
    sep_inverse,
    sep_coupling,
):
    tiles = lax.axis_size("tile")
    sections = lax.axis_size("chain")
    tile = lax.axis_index("tile")
    section = lax.axis_index("chain")
    core = tile % 2
    rows, columns = sep_rhs.shape[1:]
    half = columns // 2
    width = columns // tiles

    def of_core(block, which):
        split = block.reshape(rows, tiles // 2, 2, width)
        return jnp.where(which == 0, split[:, :, 0], split[:, :, 1]).reshape(rows, half)

    inverse_tiles = leaf_inverse[0]
    solved_free = jnp.einsum("lij,ljr->lir", inverse_tiles, leaf_rhs[0], precision=PRECISION)
    gain_tiles = jnp.einsum("lij,ljk->lik", inverse_tiles, leaf_coupling[0], precision=PRECISION)
    masked_update = leaf_update[0] * update_pattern[0].astype(jnp.float32)[:, None, None]
    local_sum = jnp.einsum("lij,ljr->ir", masked_update, solved_free, precision=PRECISION)
    local_cross = jnp.einsum("lij,ljk->ik", masked_update, gain_tiles, precision=PRECISION)

    total = jnp.concatenate([of_core(local_sum, core), local_cross], 1)
    total = total + swapped(jnp.concatenate([of_core(local_sum, 1 - core), local_cross], 1), "tile", 1)
    bit = 2
    while bit < tiles:
        total = total + swapped(total, "tile", bit)
        bit *= 2
    right = jnp.concatenate([of_core(sep_rhs[0], core), sep_coupling[0]], 1)
    solved = product(sep_inverse[0], right - total)
    offset, step_map = solved[:, :half], -solved[:, half:]

    whole_b, whole_a = offset, step_map
    before_b, before_a = jnp.zeros_like(offset), jnp.eye(rows, dtype=offset.dtype)
    bit = 1
    while bit < sections:
        last = 2 * bit >= sections
        upper = (section // bit) % 2 == 1
        if last:
            other_b = swapped(whole_b, "chain", bit)
        else:
            other = swapped(jnp.concatenate([whole_b, whole_a], 1), "chain", bit)
            other_b, other_a = other[:, :half], other[:, half:]
        if bit == 1:
            stepped = other_b
        else:
            stepped = before_b + product(before_a, other_b)
        before_b = jnp.where(upper, stepped, before_b)
        if not last:
            if bit == 1:
                stepped = other_a
            else:
                stepped = product(before_a, other_a)
            before_a = jnp.where(upper, stepped, before_a)
            first_b = jnp.where(upper, other_b, whole_b)
            first_a = jnp.where(upper, other_a, whole_a)
            second_b = jnp.where(upper, whole_b, other_b)
            second_a = jnp.where(upper, whole_a, other_a)
            whole_b = second_b + product(second_a, first_b)
            if 4 * bit < sections:
                whole_a = product(second_a, first_a)
        bit *= 2
    carry_half = before_b

    sep_half = product(step_map, carry_half) + offset
    sep_share = lax.dynamic_slice_in_dim(sep_half, (tile // 2) * width, width, 1)
    other_half = swapped(carry_half, "tile", 1)
    pieces = [h.reshape(rows, tiles // 2, 1, width) for h in (carry_half, other_half)]
    carry = jnp.where(core == 0, jnp.concatenate(pieces, 2), jnp.concatenate(pieces[::-1], 2))
    carry = carry.reshape(rows, columns)
    leaf_values = solved_free - jnp.einsum("lik,kr->lir", gain_tiles, carry, precision=PRECISION)
    return (leaf_values[None], sep_share[None])


def solution(mesh):
    return jax.shard_map(
        shards,
        mesh=mesh,
        in_specs=(
            P(("parts", "chain"), "tile", None, None),
            P(("parts", "chain"), "tile", None, None),
            P(("parts", "chain"), "tile", None, None),
            P(("parts", "chain"), "tile", None, None),
            P(("parts", "chain"), "tile"),
            P(("parts", "chain"), None, None),
            P(("parts", "chain"), None, None),
            P(("parts", "chain"), None, None),
        ),
        out_specs=(P(("parts", "chain"), "tile", None, None), P(("parts", "chain"), None, "tile")),
        check_vma=False,
    )
```

time: 98.6 us -> 56.6 us (0.57)
  waiting for transfers between devices: 47.5 us -> 16.4 us
  between operations: 14.2 us -> 0.84 us
  local copies, waits for them, and re-layouts: 1.22 us -> 8.54 us
  starting transfers between devices: 12.2 us -> 7.96 us
    psum x1 -> x0, waiting for transfers between devices: 35.3 us -> none  [shards(): total_sum, total_cross = lax.psum((local_sum, local_cross), 'tile')]
    dot_general x0 -> x1, local copies, waits for them, and re-layouts: none -> 5.97 us  [shards(): jnp.einsum('lij,ljr->ir', masked_update, solved_free, precision=PRECISION)]
    ppermute x3 -> x5, starting transfers between devices: 12.2 us -> 7.96 us  [swapped(): return lax.ppermute(block, axis, route)]
    ppermute x3 -> x5, waiting for transfers between devices: 12.2 us -> 16.4 us  [swapped(): return lax.ppermute(block, axis, route)]
    dot_general x11 -> x9, matrix products: 22.3 us -> 22.4 us  [the longest x1 6.17 us: shards(): jnp.einsum('lij,ljr->lir', inverse_tiles, leaf_rhs[0], precision=PRECISION)]
  transfers between devices with their start and end apart: 4 -> 5, of which waited for: 4 -> 5; matrix products, arithmetic and copies ran while one was open for 0% -> 2% of each run, Pallas kernels for 0% -> 0%
where the time goes in v1:
time: 56.6 us; the launch traced here: 56.3 us
  matrix products  22.4 us (40%)
  waiting for transfers between devices  16.4 us (29%)
  local copies, waits for them, and re-layouts  8.54 us (15%)
  starting transfers between devices  7.96 us (14%)
  between operations  0.84 us (1%)
    ppermute x5, waiting for transfers between devices, swapped(): return lax.ppermute(block, axis, route)  16.4 us
    ppermute x5, starting transfers between devices, swapped(): return lax.ppermute(block, axis, route)  7.96 us
    dot_general x1, matrix products, shards(): jnp.einsum('lij,ljr->lir', inverse_tiles, leaf_rhs[0], precision=PRECISION)  6.17 us
    dot_general x1, matrix products, shards(): jnp.einsum('lik,kr->lir', gain_tiles, carry, precision=PRECISION)  5.99 us
    dot_general x1, local copies, waits for them, and re-layouts, shards(): jnp.einsum('lij,ljr->ir', masked_update, solved_free, precision=PRECISION)  5.97 us
    dot_general x1, matrix products, shards(): jnp.einsum('lij,ljr->ir', masked_update, solved_free, precision=PRECISION)  5.69 us
    dot_general x1, matrix products, shards(): jnp.einsum('lij,ljk->lik', inverse_tiles, leaf_coupling[0], precision=PRE...  1.82 us
    dot_general x4, matrix products, product(): return jnp.dot(left, right, precision=PRECISION)  1.7 us
  transfers between devices with their start and end apart: 5, of which 5 were waited for; matrix products, arithmetic and copies ran while one was open for 2% of the time, Pallas kernels for 0%

profile of v1, /device:TPU:0, one launch (start us, length us, event | category | flops | bytes accessed | tf_op | source)
XLA Modules:
  0.0 56.3 jit_solution(2094104654042140022)
XLA Ops:
  0.7 1.2 %copy-done = f32[1,16,128,128]{3,2,1,0:T(8,128)S(1)} copy-done((f32[1,16,128,128]{3,2,1,0:T(8,128)S(1)}, f32[1,16,128,128]{3,2,1,0:T(8,128)}, u32[]{:S(2)}) %copy-start) | copy-done | bytes 1048600
  1.9 6.2 %fusion = f32[16,128,512]{2,1,0:T(8,128)} fusion(f32[1,16,128,512]{3,2,1,0:T(8,128)} %param.8, f32[1,16,128,128]{3,2,1,0:T(8,128)S(1)} %copy-done), kind=kOutput, calls=%fused_computation | convolution fusion | flops 805306368 | bytes 9437184 | tf_op jit(solution)/shard_map/lij,ljr->lir/dot_general | solution.py:42
  8.0 6.0 %dot_general.36 = f32[2,2,128,128,16]{2,1,0,3,4:T(2,128)} reshape(f32[512,128,16]{0,1,2:T(8,128)} %bitcast.52) | data formatting | bytes 8388608 | tf_op jit(solution)/shard_map/lij,ljr->ir/dot_general | solution.py:45
  14.0 1.8 %fusion.9 = f32[16,128,128]{2,1,0:T(8,128)S(1)} fusion(f32[1,16,128,128]{3,2,1,0:T(8,128)} %param.10, f32[1,16,128,128]{3,2,1,0:T(8,128)S(1)} %copy-done), kind=kOutput, calls=%fused_computation.12 | convolution fusion | flops 201326592 | bytes 3145728 | tf_op jit(solution)/shard_map/lij,ljk->lik/dot_general | solution.py:43
  15.9 5.7 %fusion.4 = f32[128,2,2,128]{0,3,2,1:T(8,128)S(1)} fusion(f32[2,2,128,128,16]{2,1,0,3,4:T(2,128)} %dot_general.36, f32[1,16,128,128]{3,2,1,0:T(8,128)S(1)} %copy-done.1, f32[16]{0:T(128)S(1)} %convert_bitcast_fusion), kind=kOutput, calls=%fused_computation.5 | convolution fusion | flops 805568512 | bytes 5505088 | tf_op jit(solution)/shard_map/lij,ljr->ir/dot_general | solution.py:45
  21.6 1.0 %convolution_bitcast_fusion.1 = f32[128,128]{0,1:T(8,128)S(1)} fusion(f32[16,128,128]{2,1,0:T(8,128)S(1)} %fusion.9, f32[1,16,128,128]{3,2,1,0:T(8,128)S(1)} %copy-done.1, f32[16]{0:T(128)S(1)} %convert_bitcast_fusion), kind=kOutput, calls=%fused_computation.9 | convolution fusion | flops 201588736 | bytes 2162752 | tf_op jit(solution)/shard_map/lij,ljk->ik/dot_general | solution.py:46
  22.7 0.5 collective-permute-start
  23.2 0.1 copy.17
  23.4 0.8 %collective-permute-done = f32[128,384]{0,1:T(8,128)S(1)} collective-permute-done((f32[128,384]{0,1:T(8,128)S(1)}, f32[128,384]{0,1:T(8,128)S(1)}, u32[]{:S(2)}, u32[]{:S(2)}) %collective-permute-start) | collective-permute-done | bytes 196640 | tf_op jit(solution)/shard_map/ppermute | solution.py:11
  24.3 3.0 %collective-permute-start.1 = (f32[128,384]{0,1:T(8,128)S(1)}, f32[128,384]{0,1:T(8,128)S(1)}, u32[]{:S(2)}, u32[]{:S(2)}) collective-permute-start(f32[128,384]{0,1:T(8,128)S(1)} %fusion.15), channel_id=1, source_target_pairs={{0,2},{1,3},{2,0},{3,1},{4,6},{5,7},{6,4},{7,5},{8,10},{9,11},{10,... | collective-permute-start | bytes 589832 | tf_op jit(solution)/shard_map/ppermute | solution.py:11
  27.2 5.2 %collective-permute-done.1 = f32[128,384]{0,1:T(8,128)S(1)} collective-permute-done((f32[128,384]{0,1:T(8,128)S(1)}, f32[128,384]{0,1:T(8,128)S(1)}, u32[]{:S(2)}, u32[]{:S(2)}) %collective-permute-start.1) | collective-permute-done | bytes 196640 | tf_op jit(solution)/shard_map/ppermute | solution.py:11
  32.4 1.1 %convolution_bitcast_fusion = f32[128,384]{0,1:T(8,128)S(1)} fusion(f32[128,128]{0,1:T(8,128)S(1)} %copy.18, f32[128,256]{0,1:T(8,128)S(1)} %bitcast.56, f32[128,384]{0,1:T(8,128)S(1)} %fusion.15, f32[128,384]{0,1:T(8,128)S(1)} %collective-permute-done.1, f32[1,128,128]{2,1,0:T(8,128)} %param.14), kind=kOutput, calls=%fused_computation.6 | convolution fusion | flops 37896192 | bytes 851968 | tf_op jit(solution)/shard_map/dot_general | solution.py:15
  33.6 1.9 %collective-permute-start.2 = (f32[128,384]{0,1:T(8,128)S(1)}, f32[128,384]{0,1:T(8,128)S(1)}, u32[]{:S(2)}, u32[]{:S(2)}) collective-permute-start(f32[128,384]{0,1:T(8,128)S(1)} %pad_maximum_fusion.2), channel_id=1, source_target_pairs={{0,4},{4,0},{8,12},{12,8},{1,5},{5,1},{9,13},{13,9},{2,6},{6,2},{1... | collective-permute-start | bytes 589832 | tf_op jit(solution)/shard_map/ppermute | solution.py:11
  35.4 4.6 %collective-permute-done.2 = f32[128,384]{0,1:T(8,128)S(1)} collective-permute-done((f32[128,384]{0,1:T(8,128)S(1)}, f32[128,384]{0,1:T(8,128)S(1)}, u32[]{:S(2)}, u32[]{:S(2)}) %collective-permute-start.2) | collective-permute-done | bytes 196640 | tf_op jit(solution)/shard_map/ppermute | solution.py:11
  40.1 0.2 select_add_fusion
  40.3 2.6 %collective-permute-start.3 = (f32[128,256]{0,1:T(8,128)S(1)}, f32[128,256]{0,1:T(8,128)S(1)}, u32[]{:S(2)}, u32[]{:S(2)}) collective-permute-start(f32[128,256]{0,1:T(8,128)S(1)} %select_add_fusion), channel_id=1, source_target_pairs={{0,8},{4,12},{8,0},{12,4},{1,9},{5,13},{9,1},{13,5},{2,10},{6,14},... | collective-permute-start | bytes 393224 | tf_op jit(solution)/shard_map/ppermute | solution.py:11
  42.9 5.3 %collective-permute-done.3 = f32[128,256]{0,1:T(8,128)S(1)} collective-permute-done((f32[128,256]{0,1:T(8,128)S(1)}, f32[128,256]{0,1:T(8,128)S(1)}, u32[]{:S(2)}, u32[]{:S(2)}) %collective-permute-start.3) | collective-permute-done | bytes 131104 | tf_op jit(solution)/shard_map/ppermute | solution.py:11
  48.2 0.2 fusion.7
  48.5 0.2 fusion.35
  48.7 0.7 %copy.24 = f32[128,128]{1,0:T(8,128)} copy(f32[128,128]{0,1:T(8,128)S(1)} %dynamic-slice_add_fusion) | data formatting | bytes 131072 | tf_op jit(solution)/shard_map/dynamic_slice | solution.py:91
  49.5 0.4 collective-permute-done.4
  49.9 0.2 copy.22
  50.0 0.2 reshape.44
  50.3 6.0 %subtract_bitcast_fusion = f32[1,16,128,512]{3,2,1,0:T(8,128)} fusion(f32[16,128,512]{2,1,0:T(8,128)} %fusion, f32[16,128,128]{2,1,0:T(8,128)S(1)} %fusion.9, f32[128,512,1]{1,0,2:T(8,128)S(1)} %reshape.44), kind=kOutput, calls=%fused_computation.4 | convolution fusion | flops 806354944 | bytes 9699328 | tf_op jit(solution)/shard_map/lik,kr->lir/dot_general | solution.py:96
  (21 shorter events, 0.3 us)
Async XLA Ops:
  0.6 1.2 %copy-start = (f32[1,16,128,128]{3,2,1,0:T(8,128)S(1)}, f32[1,16,128,128]{3,2,1,0:T(8,128)}, u32[]{:S(2)}) copy-start(f32[1,16,128,128]{3,2,1,0:T(8,128)} %param.9) | copy-start | bytes 3145732
  8.0 6.0 %copy-start.4 = (s32[1,16]{1,0:T(1,128)S(1)}, s32[1,16]{1,0:T(1,128)}, u32[]{:S(2)}) copy-start(s32[1,16]{1,0:T(1,128)} %param.12) | copy-start | bytes 196
  8.0 7.8 %copy-start.1 = (f32[1,16,128,128]{3,2,1,0:T(8,128)S(1)}, f32[1,16,128,128]{3,2,1,0:T(8,128)}, u32[]{:S(2)}) copy-start(f32[1,16,128,128]{3,2,1,0:T(8,128)} %param.11) | copy-start | bytes 3145732
  15.8 7.3 %copy-start.2 = (f32[1,128,512]{2,1,0:T(8,128)S(1)}, f32[1,128,512]{2,1,0:T(8,128)}, u32[]{:S(2)}) copy-start(f32[1,128,512]{2,1,0:T(8,128)} %param.13) | copy-start | bytes 786436
  15.9 7.5 %copy-start.3 = (f32[1,128,128]{2,1,0:T(8,128)S(1)}, f32[1,128,128]{2,1,0:T(8,128)}, u32[]{:S(2)}) copy-start(f32[1,128,128]{2,1,0:T(8,128)} %param.15) | copy-start | bytes 196612
  22.7 1.6 %collective-permute-start = (f32[128,384]{0,1:T(8,128)S(1)}, f32[128,384]{0,1:T(8,128)S(1)}, u32[]{:S(2)}, u32[]{:S(2)}) collective-permute-start(f32[128,384]{0,1:T(8,128)S(1)} %pad_maximum_fusion), channel_id=1, source_target_pairs={{0,1},{1,0},{2,3},{3,2},{4,5},{5,4},{6,7},{7,6},{8,9},{9,8},{10,11... | collective-permute-start | bytes 589832 | tf_op jit(solution)/shard_map/ppermute | solution.py:11
  24.3 8.2 %collective-permute-start.1 = (f32[128,384]{0,1:T(8,128)S(1)}, f32[128,384]{0,1:T(8,128)S(1)}, u32[]{:S(2)}, u32[]{:S(2)}) collective-permute-start(f32[128,384]{0,1:T(8,128)S(1)} %fusion.15), channel_id=1, source_target_pairs={{0,2},{1,3},{2,0},{3,1},{4,6},{5,7},{6,4},{7,5},{8,10},{9,11},{10,... | collective-permute-start | bytes 589832 | tf_op jit(solution)/shard_map/ppermute | solution.py:11
  33.6 6.5 %collective-permute-start.2 = (f32[128,384]{0,1:T(8,128)S(1)}, f32[128,384]{0,1:T(8,128)S(1)}, u32[]{:S(2)}, u32[]{:S(2)}) collective-permute-start(f32[128,384]{0,1:T(8,128)S(1)} %pad_maximum_fusion.2), channel_id=1, source_target_pairs={{0,4},{4,0},{8,12},{12,8},{1,5},{5,1},{9,13},{13,9},{2,6},{6,2},{1... | collective-permute-start | bytes 589832 | tf_op jit(solution)/shard_map/ppermute | solution.py:11
  40.3 7.9 %collective-permute-start.3 = (f32[128,256]{0,1:T(8,128)S(1)}, f32[128,256]{0,1:T(8,128)S(1)}, u32[]{:S(2)}, u32[]{:S(2)}) collective-permute-start(f32[128,256]{0,1:T(8,128)S(1)} %select_add_fusion), channel_id=1, source_target_pairs={{0,8},{4,12},{8,0},{12,4},{1,9},{5,13},{9,1},{13,5},{2,10},{6,14},... | collective-permute-start | bytes 393224 | tf_op jit(solution)/shard_map/ppermute | solution.py:11
  48.4 1.4 %collective-permute-start.4 = (f32[128,256]{0,1:T(8,128)S(1)}, f32[128,256]{0,1:T(8,128)S(1)}, u32[]{:S(2)}, u32[]{:S(2)}) collective-permute-start(f32[128,256]{0,1:T(8,128)S(1)} %fusion.7), channel_id=1, source_target_pairs={{0,1},{1,0},{2,3},{3,2},{4,5},{5,4},{6,7},{7,6},{8,9},{9,8},{10,11... | collective-permute-start | bytes 393224 | tf_op jit(solution)/shard_map/ppermute | solution.py:11

commit v2 on v0

v2 whole, which is shorter than its diff:
```python
import functools

import jax
import jax.numpy as jnp
from jax import lax
from jax.experimental import pallas as pl
from jax.experimental.pallas import tpu as pltpu
from jax.sharding import PartitionSpec as P

F32 = jnp.float32
BF16 = jnp.bfloat16
LANES = 128
VMEM = pltpu.MemorySpace.VMEM
IN_VMEM = pl.BlockSpec(memory_space=pltpu.VMEM)
IN_HBM = pl.BlockSpec(memory_space=pl.ANY)
GROUP = 4


def swapped(block, axis, bit):
    route = [(i, i ^ bit) for i in range(lax.axis_size(axis))]
    return lax.ppermute(block, axis, route)


def parts_of(block):
    high = block.astype(BF16)
    return high, (block - high.astype(F32)).astype(BF16)


def matmul(left, right):
    return lax.dot_general(left, right, (((1,), (0,)), ((), ())), preferred_element_type=F32)


def left_of(block):
    high, low = parts_of(block)
    return jnp.concatenate([high, low, high], 1)


def right_of(block):
    high, low = parts_of(block)
    return jnp.concatenate([high, high, low], 0)


def product(left, right):
    return matmul(left_of(left), right_of(right))


def starts(tiles, which):
    if tiles == 4:
        return [which * LANES, which * LANES + 2 * LANES]
    return [which * 2 * LANES, which * 2 * LANES + LANES]


def lanes(start):
    return pl.ds(pl.multiple_of(start, LANES), LANES)


def reduce_kernel(tiles, pattern, rhs, inverse, coupling, update, sent, kept, highs, lows, inverses, right, tiles_a, tiles_b, sems):
    leaves = rhs.shape[0]
    rows = rhs.shape[1]
    core = lax.rem(lax.axis_index("tile"), 2)
    order = starts(tiles, 1 - core) + starts(tiles, core)
    copies = []
    for k in range(leaves // GROUP):
        some = pl.ds(k * GROUP, GROUP)
        pair = [
            pltpu.make_async_copy(update.at[some], tiles_a.at[some], sems.at[k, 0]),
            pltpu.make_async_copy(inverse.at[some], tiles_b.at[some], sems.at[k, 1]),
        ]
        for copy in pair:
            copy.start()
        copies.append(pair)
    blocks = []
    for k in range(leaves // GROUP):
        some = pl.ds(k * GROUP, GROUP)
        row = []
        for j, start in enumerate(order):
            place = j * LANES if j < 2 else (j + 1) * LANES
            row.append(pltpu.make_async_copy(rhs.at[some, :, lanes(start)], right.at[some, :, pl.ds(place, LANES)], sems.at[k, 2 + j]))
        row.append(pltpu.make_async_copy(coupling.at[some], right.at[some, :, pl.ds(2 * LANES, LANES)], sems.at[k, 6]))
        for copy in row:
            copy.start()
        blocks.append(row)
    lefts = []
    for k in range(leaves // GROUP):
        for copy in copies[k]:
            copy.wait()
        for leaf in range(k * GROUP, k * GROUP + GROUP):
            inv_high, inv_low = parts_of(tiles_b[leaf])
            inverses[leaf] = jnp.concatenate([inv_high, inv_low, inv_high], 1)
            masked = tiles_a[leaf] * pattern[0, leaf].astype(F32)
            lefts.append(left_of(matmul(left_of(masked), jnp.concatenate([inv_high, inv_high, inv_low], 0))))
    total = None
    for k in range(leaves // GROUP):
        for copy in blocks[k]:
            copy.wait()
        stacked = []
        for leaf in range(k * GROUP, k * GROUP + GROUP):
            high, low = parts_of(right[leaf])
            highs[leaf] = high
            lows[leaf] = low
            stacked += [high, high, low]
        here = matmul(jnp.concatenate(lefts[k * GROUP : k * GROUP + GROUP], 1), jnp.concatenate(stacked, 0))
        total = here if total is None else total + here
    sent[...] = total[:, : 3 * LANES]
    kept[:, : 2 * LANES] = total[:, 3 * LANES :]
    kept[:, 2 * LANES :] = total[:, 2 * LANES : 3 * LANES]


def reduced(tiles, pattern, rhs, inverse, coupling, update):
    leaves, rows, columns = rhs.shape
    wide = columns + rows
    return pl.pallas_call(
        functools.partial(reduce_kernel, tiles),
        out_shape=(
            VMEM((rows, columns // 2 + rows), F32),
            VMEM((rows, columns // 2 + rows), F32),
            VMEM((leaves, rows, wide), BF16),
            VMEM((leaves, rows, wide), BF16),
            VMEM((leaves, rows, 3 * rows), BF16),
        ),
        in_specs=[pl.BlockSpec(memory_space=pltpu.SMEM)] + [IN_HBM] * 4,
        out_specs=(IN_VMEM,) * 5,
        scratch_shapes=[
            pltpu.VMEM((leaves, rows, wide), F32),
            pltpu.VMEM((leaves, rows, rows), F32),
            pltpu.VMEM((leaves, rows, rows), F32),
            pltpu.SemaphoreType.DMA((leaves // GROUP, 7)),
        ],
        compiler_params=pltpu.CompilerParams(vmem_limit_bytes=50 << 20),
    )(pattern, rhs, inverse, coupling, update)


def free_kernel(highs, lows, inverses, solved, gains):
    for leaf in range(highs.shape[0]):
        high = highs[leaf]
        here = matmul(inverses[leaf], jnp.concatenate([high, high, lows[leaf]], 0))
        solved[leaf, :, : 2 * LANES] = here[:, : 2 * LANES]
        solved[leaf, :, 2 * LANES :] = here[:, 3 * LANES :]
        gains[leaf] = left_of(here[:, 2 * LANES : 3 * LANES])


def freed(highs, lows, inverses):
    leaves, rows, wide = highs.shape
    columns = wide - rows
    return pl.pallas_call(
        free_kernel,
        out_shape=(VMEM((leaves, rows, columns), F32), VMEM((leaves, rows, 3 * rows), BF16)),
        in_specs=[IN_VMEM] * 3,
        out_specs=(IN_VMEM,) * 2,
        compiler_params=pltpu.CompilerParams(vmem_limit_bytes=20 << 20),
        cost_estimate=pl.CostEstimate(flops=6 * leaves * rows * rows * wide, bytes_accessed=leaves * rows * wide * 8, transcendentals=0),
    )(highs, lows, inverses)


def section_kernel(tiles, received, kept, sep_rhs, sep_inverse, sep_coupling, solved):
    core = lax.rem(lax.axis_index("tile"), 2)
    first, second = starts(tiles, core)
    right = jnp.concatenate([sep_rhs[:, lanes(first)], sep_rhs[:, lanes(second)], sep_coupling[...]], 1)
    solved[...] = product(sep_inverse[...], right - (received[...] + kept[...]))


def section_map(tiles, received, kept, sep_rhs, sep_inverse, sep_coupling):
    return pl.pallas_call(
        functools.partial(section_kernel, tiles),
        out_shape=VMEM(kept.shape, F32),
        in_specs=[IN_VMEM] * 5,
        out_specs=IN_VMEM,
    )(received, kept, sep_rhs, sep_inverse, sep_coupling)


def pair_kernel(mine, other, whole):
    half = whole.shape[1]

    @pl.when(lax.rem(lax.axis_index("chain"), 2) == 1)
    def _():
        whole[...] = mine[:, :half] - product(mine[:, half:], other[:, :half])

    @pl.when(lax.rem(lax.axis_index("chain"), 2) == 0)
    def _():
        whole[...] = other[:, :half] - product(other[:, half:], mine[:, :half])


def paired(mine, other, half):
    return pl.pallas_call(
        pair_kernel,
        out_shape=VMEM((mine.shape[0], half), F32),
        in_specs=[IN_VMEM] * 2,
        out_specs=IN_VMEM,
    )(mine, other)


def carry_kernel(other, received, carry):
    half = carry.shape[1]
    section = lax.axis_index("chain")

    @pl.when(section == 0)
    def _():
        carry[...] = jnp.zeros_like(carry)

    @pl.when(section == 1)
    def _():
        carry[...] = other[:, :half]

    @pl.when(section == 2)
    def _():
        carry[...] = received[...]

    @pl.when(section == 3)
    def _():
        carry[...] = other[:, :half] - product(other[:, half:], received[...])


def carried(other, received):
    return pl.pallas_call(
        carry_kernel,
        out_shape=VMEM(received.shape, F32),
        in_specs=[IN_VMEM] * 2,
        out_specs=IN_VMEM,
    )(other, received)


def affine_kernel(step, block, offset, result):
    result[...] = offset[...] - product(step[...], block[...])


def affine(step, block, offset):
    return pl.pallas_call(
        affine_kernel,
        out_shape=VMEM(offset.shape, F32),
        in_specs=[IN_VMEM] * 3,
        out_specs=IN_VMEM,
    )(step, block, offset)


def scanned(section, solved, half):
    sections = lax.axis_size("chain")
    whole_b, whole_a = solved[:, :half], solved[:, half:]
    before_b, before_a = jnp.zeros_like(whole_b), -jnp.eye(whole_a.shape[0], dtype=F32)
    nothing = jnp.zeros_like(whole_a)
    bit = 1
    while bit < sections:
        upper = (section // bit) % 2 == 1
        other = swapped(jnp.concatenate([whole_b, whole_a], 1), "chain", bit)
        other_b, other_a = other[:, :half], other[:, half:]
        before_b = jnp.where(upper, affine(before_a, other_b, before_b), before_b)
        before_a = jnp.where(upper, affine(before_a, other_a, nothing), before_a)
        first_b, first_a = jnp.where(upper, other_b, whole_b), jnp.where(upper, other_a, whole_a)
        second_b, second_a = jnp.where(upper, whole_b, other_b), jnp.where(upper, whole_a, other_a)
        whole_b = affine(second_a, first_b, second_b)
        whole_a = affine(second_a, first_a, nothing)
        bit *= 2
    return before_b


def last_kernel(tiles, solved, gains, theirs, mine, out, values, sems):
    leaves = solved.shape[0]
    core = lax.rem(lax.axis_index("tile"), 2)
    order = starts(tiles, 1 - core) + starts(tiles, core)
    right = jnp.concatenate([right_of(theirs[...]), right_of(mine[...])], 1)
    copies = []
    for k in range(leaves // GROUP):
        for leaf in range(k * GROUP, k * GROUP + GROUP):
            values[leaf] = solved[leaf] - matmul(gains[leaf], right)
        some = pl.ds(k * GROUP, GROUP)
        for j, start in enumerate(order):
            copy = pltpu.make_async_copy(values.at[some, :, pl.ds(j * LANES, LANES)], out.at[some, :, lanes(start)], sems.at[k, j])
            copy.start()
            copies.append(copy)
    for copy in copies:
        copy.wait()


def leaf_values(tiles, solved, gains, theirs, mine):
    return pl.pallas_call(
        functools.partial(last_kernel, tiles),
        out_shape=jax.ShapeDtypeStruct(solved.shape, F32),
        in_specs=[IN_VMEM] * 4,
        out_specs=IN_HBM,
        scratch_shapes=[pltpu.VMEM(solved.shape, F32), pltpu.SemaphoreType.DMA((solved.shape[0] // GROUP, 4))],
        compiler_params=pltpu.CompilerParams(vmem_limit_bytes=20 << 20),
    )(solved, gains, theirs, mine)


def shards(
    leaf_rhs,
    leaf_inverse,
    leaf_coupling,
    leaf_update,
    update_pattern,
    sep_rhs,
    sep_inverse,
    sep_coupling,
):
    tiles = lax.axis_size("tile")
    sections = lax.axis_size("chain")
    tile = lax.axis_index("tile")
    section = lax.axis_index("chain")
    columns = sep_rhs.shape[2]
    half = columns // 2
    width = columns // tiles

    sent, kept, highs, lows, inverses = reduced(tiles, update_pattern, leaf_rhs[0], leaf_inverse[0], leaf_coupling[0], leaf_update[0])
    kept = kept + swapped(sent, "tile", 1)
    received = swapped(kept, "tile", 2) if tiles > 2 else jnp.zeros_like(kept)
    bit = 4
    while bit < tiles:
        kept = kept + received
        received = swapped(kept, "tile", bit)
        bit *= 2
    solved, gains = freed(highs, lows, inverses)
    mapped = section_map(tiles, received, kept, sep_rhs[0], sep_inverse[0], sep_coupling[0])
    if sections == 4:
        other = swapped(mapped, "chain", 1)
        whole = paired(mapped, other, half)
        carry = carried(other, swapped(whole, "chain", 2))
    else:
        carry = scanned(section, mapped, half)
    theirs = swapped(carry, "tile", 1)
    sep_values = affine(mapped[:, half:], carry, mapped[:, :half])
    if tiles == 4:
        sep_share = lax.dynamic_slice_in_dim(sep_values, (tile // 2) * width, width, 1)
    else:
        other_values = swapped(sep_values, "tile", 1)
        lower = jnp.where(tile % 2 == 0, sep_values, other_values)
        upper = jnp.where(tile % 2 == 0, other_values, sep_values)
        sep_share = lax.dynamic_slice_in_dim(jnp.concatenate([lower, upper], 1), tile * width, width, 1)
    return (leaf_values(tiles, solved, gains, theirs, carry)[None], sep_share[None])


def solution(mesh):
    return jax.shard_map(
        shards,
        mesh=mesh,
        in_specs=(
            P(("parts", "chain"), "tile", None, None),
            P(("parts", "chain"), "tile", None, None),
            P(("parts", "chain"), "tile", None, None),
            P(("parts", "chain"), "tile", None, None),
            P(("parts", "chain"), "tile"),
            P(("parts", "chain"), None, None),
            P(("parts", "chain"), None, None),
            P(("parts", "chain"), None, None),
        ),
        out_specs=(P(("parts", "chain"), "tile", None, None), P(("parts", "chain"), None, "tile")),
        check_vma=False,
    )
```

time: 98.6 us -> 57.3 us (0.58)
  waiting for transfers between devices: 47.5 us -> 16.3 us
  matrix products: 22.3 us -> 0 us
  local copies, waits for them, and re-layouts: 1.22 us -> 17.4 us
  Pallas kernels: 0 us -> 14.6 us
  between operations: 14.2 us -> 0.76 us
  starting transfers between devices: 12.2 us -> 7.87 us
    psum x1 -> x0, waiting for transfers between devices: 35.3 us -> none  [shards(): total_sum, total_cross = lax.psum((local_sum, local_cross), 'tile')]
    dot_general x11 -> x0, matrix products: 22.3 us -> none  [the longest x1 6.52 us: shards(): jnp.einsum('lik,kr->lir', gain_tiles, carry_in, precision=highest)]
    unnamed x14 -> x32, local copies, waits for them, and re-layouts: 0.49 us -> 15.5 us
    pallas_call x0 -> x7, Pallas kernels: none -> 14.6 us  [the longest x1 5.37 us: reduced(): pl.pallas_call(functools.partial(reduce_kernel, tiles), out_shape=(VMEM((...]
    ppermute x3 -> x5, starting transfers between devices: 12.2 us -> 7.87 us  [swapped(): return lax.ppermute(block, axis, route)]
    ppermute x3 -> x5, waiting for transfers between devices: 12.2 us -> 16.3 us  [swapped(): return lax.ppermute(block, axis, route)]
    slice x0 -> x2, local copies, waits for them, and re-layouts: none -> 1.31 us  [shards(): sep_values = affine(mapped[:, half:], carry, mapped[:, :half])]
  transfers between devices with their start and end apart: 4 -> 5, of which waited for: 4 -> 4; matrix products, arithmetic and copies ran while one was open for 0% -> 3% of each run, Pallas kernels for 0% -> 5%
where the time goes in v2:
time: 57.3 us; the launch traced here: 56.9 us
  local copies, waits for them, and re-layouts  17.4 us (30%)
  waiting for transfers between devices  16.3 us (28%)
  Pallas kernels  14.6 us (25%)
  starting transfers between devices  7.87 us (14%)
  between operations  0.76 us (1%)
    ppermute x5, waiting for transfers between devices, swapped(): return lax.ppermute(block, axis, route)  16.3 us
    unnamed x32, local copies, waits for them, and re-layouts  15.5 us
    ppermute x5, starting transfers between devices, swapped(): return lax.ppermute(block, axis, route)  7.87 us
    pallas_call x1, Pallas kernels, reduced(): pl.pallas_call(functools.partial(reduce_kernel, tiles), out_shape=(VMEM((...  5.37 us
    pallas_call x1, Pallas kernels, leaf_values(): pl.pallas_call(functools.partial(last_kernel, tiles), out_shape=jax.Shape...  2.57 us
    pallas_call x1, Pallas kernels, freed(): pl.pallas_call(free_kernel, out_shape=(VMEM((leaves, rows, columns), F32)...  1.81 us
    pallas_call x1, Pallas kernels, section_map(): pl.pallas_call(functools.partial(section_kernel, tiles), out_shape=VMEM(k...  1.41 us
    slice x2, local copies, waits for them, and re-layouts, shards(): sep_values = affine(mapped[:, half:], carry, mapped[:, :half])  1.31 us
  transfers between devices with their start and end apart: 5, of which 4 were waited for; matrix products, arithmetic and copies ran while one was open for 3% of the time, Pallas kernels for 5%

profile of v2, /device:TPU:0, one launch (start us, length us, event | category | flops | bytes accessed | tf_op | source)
XLA Modules:
  0.0 56.9 jit_solution(12314321378325447426)
XLA Ops:
  0.6 5.4 %shard_map.95 = (f32[128,384]{1,0:T(8,128)S(1)}, f32[128,384]{1,0:T(8,128)S(1)}, bf16[16,128,640]{2,1,0:T(8,128)(2,1)S(1)}, bf16[16,128,640]{2,1,0:T(8,128)(2,1)S(1)}, bf16[16,128,384]{2,1,0:T(8,128)(2,1)S(1)}) custom-call(s32[1,16]{1,0:T(1,128)} %pattern.1, f32[16,128,512]{2,1,0:T(8,128)} %bitcast.10, f32[16,128,128]{2,1,0:T(8,128)} %bitcast.12, ...), custom_call_target="tpu_custom_call" | custom-call | tf_op jit(solution)/shard_map/pallas_call | solution.py:112
  6.0 1.5 %copy-done.2 = bf16[16,128,640]{2,1,0:T(8,128)(2,1)} copy-done((bf16[16,128,640]{2,1,0:T(8,128)(2,1)}, bf16[16,128,640]{2,1,0:T(8,128)(2,1)S(1)}, u32[]{:S(2)}) %copy-start.2) | copy-done | bytes 2621464
  7.5 1.2 %copy-done.8 = bf16[16,128,384]{2,1,0:T(8,128)(2,1)} copy-done((bf16[16,128,384]{2,1,0:T(8,128)(2,1)}, bf16[16,128,384]{2,1,0:T(8,128)(2,1)S(1)}, u32[]{:S(2)}) %copy-start.8) | copy-done | bytes 1572888
  9.1 1.1 %collective-permute-done = f32[128,384]{1,0:T(8,128)S(1)} collective-permute-done((f32[128,384]{1,0:T(8,128)S(1)}, f32[128,384]{1,0:T(8,128)S(1)}, u32[]{:S(2)}, u32[]{:S(2)}) %collective-permute-start) | collective-permute-done | bytes 196640 | tf_op jit(solution)/shard_map/ppermute | solution.py:21
  10.2 3.0 %collective-permute-start.1 = (f32[128,384]{1,0:T(8,128)S(1)}, f32[128,384]{1,0:T(8,128)S(1)}, u32[]{:S(2)}, u32[]{:S(2)}) collective-permute-start(f32[128,384]{1,0:T(8,128)S(1)} %add.7.kept), channel_id=1, source_target_pairs={{0,2},{1,3},{2,0},{3,1},{4,6},{5,7},{6,4},{7,5},{8,10},{9,11},{10,... | collective-permute-start | bytes 589832 | tf_op jit(solution)/shard_map/ppermute | solution.py:21
  13.2 5.2 %collective-permute-done.1.received = f32[128,384]{1,0:T(8,128)S(1)} collective-permute-done((f32[128,384]{1,0:T(8,128)S(1)}, f32[128,384]{1,0:T(8,128)S(1)}, u32[]{:S(2)}, u32[]{:S(2)}) %collective-permute-start.1) | collective-permute-done | bytes 196640 | tf_op jit(solution)/shard_map/ppermute | solution.py:21
  19.1 1.4 %shard_map.97.mine = f32[128,384]{1,0:T(8,128)S(1)} custom-call(f32[128,384]{1,0:T(8,128)} %copy-done.14, f32[128,384]{1,0:T(8,128)} %copy-done.13, f32[128,512]{1,0:T(8,128)} %bitcast.15, f32[128,128]{1,0:T(8,128)} %bitcast.16, f32[128,128]{1,0:T(8,128)} %bitcast.17), custom_call_target="tpu_custom_call" | custom-call | tf_op jit(solution)/shard_map/pallas_call | solution.py:163
  20.5 1.9 %collective-permute-start.2 = (f32[128,384]{1,0:T(8,128)S(1)}, f32[128,384]{1,0:T(8,128)S(1)}, u32[]{:S(2)}, u32[]{:S(2)}) collective-permute-start(f32[128,384]{1,0:T(8,128)S(1)} %shard_map.97.mine), channel_id=1, source_target_pairs={{0,4},{4,0},{8,12},{12,8},{1,5},{5,1},{9,13},{13,9},{2,6},{6,2},{1... | collective-permute-start | bytes 589832 | tf_op jit(solution)/shard_map/ppermute | solution.py:21
  22.3 4.6 %collective-permute-done.2.other = f32[128,384]{1,0:T(8,128)S(1)} collective-permute-done((f32[128,384]{1,0:T(8,128)S(1)}, f32[128,384]{1,0:T(8,128)S(1)}, u32[]{:S(2)}, u32[]{:S(2)}) %collective-permute-start.2) | collective-permute-done | bytes 196640 | tf_op jit(solution)/shard_map/ppermute | solution.py:21
  27.0 0.7 %copy-done.12 = f32[128,384]{1,0:T(8,128)} copy-done((f32[128,384]{1,0:T(8,128)}, f32[128,384]{1,0:T(8,128)S(1)}, u32[]{:S(2)}) %copy-start.12) | copy-done | bytes 196632
  27.7 1.2 %shard_map.98 = f32[128,256]{1,0:T(8,128)S(1)} custom-call(f32[128,384]{1,0:T(8,128)} %copy-done.4, f32[128,384]{1,0:T(8,128)} %copy-done.12), custom_call_target="tpu_custom_call" | custom-call | tf_op jit(solution)/shard_map/pallas_call | solution.py:184
  28.9 2.5 %collective-permute-start.3 = (f32[128,256]{1,0:T(8,128)S(1)}, f32[128,256]{1,0:T(8,128)S(1)}, u32[]{:S(2)}, u32[]{:S(2)}) collective-permute-start(f32[128,256]{1,0:T(8,128)S(1)} %shard_map.98), channel_id=1, source_target_pairs={{0,8},{4,12},{8,0},{12,4},{1,9},{5,13},{9,1},{13,5},{2,10},{6,14},... | collective-permute-start | bytes 393224 | tf_op jit(solution)/shard_map/ppermute | solution.py:21
  31.4 5.3 %collective-permute-done.3.received = f32[128,256]{1,0:T(8,128)S(1)} collective-permute-done((f32[128,256]{1,0:T(8,128)S(1)}, f32[128,256]{1,0:T(8,128)S(1)}, u32[]{:S(2)}, u32[]{:S(2)}) %collective-permute-start.3) | collective-permute-done | bytes 131104 | tf_op jit(solution)/shard_map/ppermute | solution.py:21
  37.4 1.0 %shard_map.99.mine.block = f32[128,256]{1,0:T(8,128)S(1)} custom-call(f32[128,384]{1,0:T(8,128)} %copy-done.12, f32[128,256]{1,0:T(8,128)} %copy-done.15), custom_call_target="tpu_custom_call" | custom-call | tf_op jit(solution)/shard_map/pallas_call | solution.py:214
  38.5 1.7 %copy-done.3 = bf16[16,128,640]{2,1,0:T(8,128)(2,1)S(1)} copy-done((bf16[16,128,640]{2,1,0:T(8,128)(2,1)S(1)}, bf16[16,128,640]{2,1,0:T(8,128)(2,1)}, u32[]{:S(2)}) %copy-start.3) | copy-done | bytes 2621464
  40.3 1.4 %copy-done.9 = bf16[16,128,384]{2,1,0:T(8,128)(2,1)S(1)} copy-done((bf16[16,128,384]{2,1,0:T(8,128)(2,1)S(1)}, bf16[16,128,384]{2,1,0:T(8,128)(2,1)}, u32[]{:S(2)}) %copy-start.9) | copy-done | bytes 1572888
  41.7 1.8 %shard_map.96 = (f32[16,128,512]{2,1,0:T(8,128)S(1)}, bf16[16,128,384]{2,1,0:T(8,128)(2,1)S(1)}) custom-call(bf16[16,128,640]{2,1,0:T(8,128)(2,1)S(1)} %get-tuple-element.9.highs, bf16[16,128,640]{2,1,0:T(8,128)(2,1)S(1)} %copy-done.3, bf16[16,128,384]{2,1,0:T(8,128)(2,1)S(1)} %copy-done.9), custom_call_target="tpu_custom_call" | custom-call | flops 1006632960 | bytes 10485760 | tf_op jit(solution)/shard_map/pallas_call | solution.py:145
  43.5 2.0 %copy-done = f32[16,128,512]{2,1,0:T(8,128)} copy-done((f32[16,128,512]{2,1,0:T(8,128)}, f32[16,128,512]{2,1,0:T(8,128)S(1)}, u32[]{:S(2)}) %copy-start) | copy-done | bytes 4194328
  45.5 1.2 %copy-done.6 = bf16[16,128,384]{2,1,0:T(8,128)(2,1)} copy-done((bf16[16,128,384]{2,1,0:T(8,128)(2,1)}, bf16[16,128,384]{2,1,0:T(8,128)(2,1)S(1)}, u32[]{:S(2)}) %copy-start.6) | copy-done | bytes 1572888
  48.0 1.2 %shard_map.101 = f32[128,256]{1,0:T(8,128)S(1)} custom-call(f32[128,128]{1,0:T(8,128)} %slice.8.step, f32[128,256]{1,0:T(8,128)} %copy-done.10, f32[128,256]{1,0:T(8,128)} %slice.9.offset), custom_call_target="tpu_custom_call" | custom-call | tf_op jit(solution)/shard_map/pallas_call | solution.py:227
  49.8 2.2 %copy-done.1 = f32[16,128,512]{2,1,0:T(8,128)S(1)} copy-done((f32[16,128,512]{2,1,0:T(8,128)S(1)}, f32[16,128,512]{2,1,0:T(8,128)}, u32[]{:S(2)}) %copy-start.1) | copy-done | bytes 4194328
  52.0 1.4 %copy-done.7 = bf16[16,128,384]{2,1,0:T(8,128)(2,1)S(1)} copy-done((bf16[16,128,384]{2,1,0:T(8,128)(2,1)S(1)}, bf16[16,128,384]{2,1,0:T(8,128)(2,1)}, u32[]{:S(2)}) %copy-start.7) | copy-done | bytes 1572888
  53.4 0.9 %copy-done.11 = f32[128,256]{1,0:T(8,128)S(1)} copy-done((f32[128,256]{1,0:T(8,128)S(1)}, f32[128,256]{1,0:T(8,128)}, u32[]{:S(2)}) %copy-start.11) | copy-done | bytes 131096
  54.3 2.6 %shard_map.100 = f32[16,128,512]{2,1,0:T(8,128)} custom-call(f32[16,128,512]{2,1,0:T(8,128)S(1)} %copy-done.1, bf16[16,128,384]{2,1,0:T(8,128)(2,1)S(1)} %copy-done.7, f32[128,256]{1,0:T(8,128)S(1)} %collective-permute-done.4.theirs, f32[128,256]{1,0:T(8,128)S(1)} %copy-done.11), custom_call_target="tpu_custom_call" | custom-call | tf_op jit(solution)/shard_map/pallas_call | solution.py:274
  (29 shorter events, 3.8 us)
Async XLA Ops:
  6.0 1.5 %copy-start.2 = (bf16[16,128,640]{2,1,0:T(8,128)(2,1)}, bf16[16,128,640]{2,1,0:T(8,128)(2,1)S(1)}, u32[]{:S(2)}) copy-start(bf16[16,128,640]{2,1,0:T(8,128)(2,1)S(1)} %get-tuple-element.10.lows) | copy-start | bytes 7864324
  7.5 1.2 %copy-start.8 = (bf16[16,128,384]{2,1,0:T(8,128)(2,1)}, bf16[16,128,384]{2,1,0:T(8,128)(2,1)S(1)}, u32[]{:S(2)}) copy-start(bf16[16,128,384]{2,1,0:T(8,128)(2,1)S(1)} %get-tuple-element.11.inverses) | copy-start | bytes 4718596
  8.7 1.5 %collective-permute-start = (f32[128,384]{1,0:T(8,128)S(1)}, f32[128,384]{1,0:T(8,128)S(1)}, u32[]{:S(2)}, u32[]{:S(2)}) collective-permute-start(f32[128,384]{1,0:T(8,128)S(1)} %get-tuple-element.15), channel_id=1, source_target_pairs={{0,1},{1,0},{2,3},{3,2},{4,5},{5,4},{6,7},{7,6},{8,9},{9,8},{10,11... | collective-permute-start | bytes 589832 | tf_op jit(solution)/shard_map/ppermute | solution.py:21
  10.2 8.2 %copy-start.13 = (f32[128,384]{1,0:T(8,128)}, f32[128,384]{1,0:T(8,128)S(1)}, u32[]{:S(2)}) copy-start(f32[128,384]{1,0:T(8,128)S(1)} %add.7.kept) | copy-start | bytes 589828
  10.2 8.2 %collective-permute-start.1 = (f32[128,384]{1,0:T(8,128)S(1)}, f32[128,384]{1,0:T(8,128)S(1)}, u32[]{:S(2)}, u32[]{:S(2)}) collective-permute-start(f32[128,384]{1,0:T(8,128)S(1)} %add.7.kept), channel_id=1, source_target_pairs={{0,2},{1,3},{2,0},{3,1},{4,6},{5,7},{6,4},{7,5},{8,10},{9,11},{10,... | collective-permute-start | bytes 589832 | tf_op jit(solution)/shard_map/ppermute | solution.py:21
  18.4 0.7 %copy-start.14 = (f32[128,384]{1,0:T(8,128)}, f32[128,384]{1,0:T(8,128)S(1)}, u32[]{:S(2)}) copy-start(f32[128,384]{1,0:T(8,128)S(1)} %collective-permute-done.1.received) | copy-start | bytes 589828
  20.5 6.5 %copy-start.4 = (f32[128,384]{1,0:T(8,128)}, f32[128,384]{1,0:T(8,128)S(1)}, u32[]{:S(2)}) copy-start(f32[128,384]{1,0:T(8,128)S(1)} %shard_map.97.mine) | copy-start | bytes 589828
  20.5 6.5 %collective-permute-start.2 = (f32[128,384]{1,0:T(8,128)S(1)}, f32[128,384]{1,0:T(8,128)S(1)}, u32[]{:S(2)}, u32[]{:S(2)}) collective-permute-start(f32[128,384]{1,0:T(8,128)S(1)} %shard_map.97.mine), channel_id=1, source_target_pairs={{0,4},{4,0},{8,12},{12,8},{1,5},{5,1},{9,13},{13,9},{2,6},{6,2},{1... | collective-permute-start | bytes 589832 | tf_op jit(solution)/shard_map/ppermute | solution.py:21
  27.0 0.7 %copy-start.12 = (f32[128,384]{1,0:T(8,128)}, f32[128,384]{1,0:T(8,128)S(1)}, u32[]{:S(2)}) copy-start(f32[128,384]{1,0:T(8,128)S(1)} %collective-permute-done.2.other) | copy-start | bytes 589828
  28.9 7.9 %collective-permute-start.3 = (f32[128,256]{1,0:T(8,128)S(1)}, f32[128,256]{1,0:T(8,128)S(1)}, u32[]{:S(2)}, u32[]{:S(2)}) collective-permute-start(f32[128,256]{1,0:T(8,128)S(1)} %shard_map.98), channel_id=1, source_target_pairs={{0,8},{4,12},{8,0},{12,4},{1,9},{5,13},{9,1},{13,5},{2,10},{6,14},... | collective-permute-start | bytes 393224 | tf_op jit(solution)/shard_map/ppermute | solution.py:21
  36.8 0.6 %copy-start.15 = (f32[128,256]{1,0:T(8,128)}, f32[128,256]{1,0:T(8,128)S(1)}, u32[]{:S(2)}) copy-start(f32[128,256]{1,0:T(8,128)S(1)} %collective-permute-done.3.received) | copy-start | bytes 393220
  38.4 5.1 %copy-start.10 = (f32[128,256]{1,0:T(8,128)}, f32[128,256]{1,0:T(8,128)S(1)}, u32[]{:S(2)}) copy-start(f32[128,256]{1,0:T(8,128)S(1)} %shard_map.99.mine.block) | copy-start | bytes 393220
  38.4 11.4 %collective-permute-start.4 = (f32[128,256]{1,0:T(8,128)S(1)}, f32[128,256]{1,0:T(8,128)S(1)}, u32[]{:S(2)}, u32[]{:S(2)}) collective-permute-start(f32[128,256]{1,0:T(8,128)S(1)} %shard_map.99.mine.block), channel_id=1, source_target_pairs={{0,1},{1,0},{2,3},{3,2},{4,5},{5,4},{6,7},{7,6},{8,9},{9,8},{10,11... | collective-permute-start | bytes 393224 | tf_op jit(solution)/shard_map/ppermute | solution.py:21
  38.5 1.7 %copy-start.3 = (bf16[16,128,640]{2,1,0:T(8,128)(2,1)S(1)}, bf16[16,128,640]{2,1,0:T(8,128)(2,1)}, u32[]{:S(2)}) copy-start(bf16[16,128,640]{2,1,0:T(8,128)(2,1)} %copy-done.2) | copy-start | bytes 7864324
  40.3 1.4 %copy-start.9 = (bf16[16,128,384]{2,1,0:T(8,128)(2,1)S(1)}, bf16[16,128,384]{2,1,0:T(8,128)(2,1)}, u32[]{:S(2)}) copy-start(bf16[16,128,384]{2,1,0:T(8,128)(2,1)} %copy-done.8) | copy-start | bytes 4718596
  41.7 5.0 %copy-start.5 = (f32[128,384]{1,0:T(8,128)S(1)}, f32[128,384]{1,0:T(8,128)}, u32[]{:S(2)}) copy-start(f32[128,384]{1,0:T(8,128)} %copy-done.4) | copy-start | bytes 589828
  43.5 2.0 %copy-start = (f32[16,128,512]{2,1,0:T(8,128)}, f32[16,128,512]{2,1,0:T(8,128)S(1)}, u32[]{:S(2)}) copy-start(f32[16,128,512]{2,1,0:T(8,128)S(1)} %get-tuple-element.12.solved) | copy-start | bytes 12582916
  45.5 1.2 %copy-start.6 = (bf16[16,128,384]{2,1,0:T(8,128)(2,1)}, bf16[16,128,384]{2,1,0:T(8,128)(2,1)S(1)}, u32[]{:S(2)}) copy-start(bf16[16,128,384]{2,1,0:T(8,128)(2,1)S(1)} %get-tuple-element.13.gains) | copy-start | bytes 4718596
  49.8 2.2 %copy-start.1 = (f32[16,128,512]{2,1,0:T(8,128)S(1)}, f32[16,128,512]{2,1,0:T(8,128)}, u32[]{:S(2)}) copy-start(f32[16,128,512]{2,1,0:T(8,128)} %copy-done) | copy-start | bytes 12582916
  52.0 1.4 %copy-start.7 = (bf16[16,128,384]{2,1,0:T(8,128)(2,1)S(1)}, bf16[16,128,384]{2,1,0:T(8,128)(2,1)}, u32[]{:S(2)}) copy-start(bf16[16,128,384]{2,1,0:T(8,128)(2,1)} %copy-done.6) | copy-start | bytes 4718596
  53.4 0.9 %copy-start.11 = (f32[128,256]{1,0:T(8,128)S(1)}, f32[128,256]{1,0:T(8,128)}, u32[]{:S(2)}) copy-start(f32[128,256]{1,0:T(8,128)} %copy-done.10) | copy-start | bytes 393220

commit v3 on v2

--- a/solution.py
+++ b/solution.py
@@ -14,6 +14,7 @@
 IN_VMEM = pl.BlockSpec(memory_space=pltpu.VMEM)
 IN_HBM = pl.BlockSpec(memory_space=pl.ANY)
 GROUP = 4
+SMALL = 4 << 20
 
 
 def swapped(block, axis, bit):
@@ -147,7 +148,7 @@
         out_shape=(VMEM((leaves, rows, columns), F32), VMEM((leaves, rows, 3 * rows), BF16)),
         in_specs=[IN_VMEM] * 3,
         out_specs=(IN_VMEM,) * 2,
-        compiler_params=pltpu.CompilerParams(vmem_limit_bytes=20 << 20),
+        compiler_params=pltpu.CompilerParams(vmem_limit_bytes=12 << 20),
         cost_estimate=pl.CostEstimate(flops=6 * leaves * rows * rows * wide, bytes_accessed=leaves * rows * wide * 8, transcendentals=0),
     )(highs, lows, inverses)
 
@@ -165,6 +166,7 @@
         out_shape=VMEM(kept.shape, F32),
         in_specs=[IN_VMEM] * 5,
         out_specs=IN_VMEM,
+        compiler_params=pltpu.CompilerParams(vmem_limit_bytes=SMALL),
     )(received, kept, sep_rhs, sep_inverse, sep_coupling)
 
 
@@ -186,6 +188,7 @@
         out_shape=VMEM((mine.shape[0], half), F32),
         in_specs=[IN_VMEM] * 2,
         out_specs=IN_VMEM,
+        compiler_params=pltpu.CompilerParams(vmem_limit_bytes=SMALL),
     )(mine, other)
 
 
@@ -216,6 +219,7 @@
         out_shape=VMEM(received.shape, F32),
         in_specs=[IN_VMEM] * 2,
         out_specs=IN_VMEM,
+        compiler_params=pltpu.CompilerParams(vmem_limit_bytes=SMALL),
     )(other, received)
 
 
@@ -229,6 +233,7 @@
         out_shape=VMEM(offset.shape, F32),
         in_specs=[IN_VMEM] * 3,
         out_specs=IN_VMEM,
+        compiler_params=pltpu.CompilerParams(vmem_limit_bytes=SMALL),
     )(step, block, offset)
 
 
@@ -277,7 +282,7 @@
         in_specs=[IN_VMEM] * 4,
         out_specs=IN_HBM,
         scratch_shapes=[pltpu.VMEM(solved.shape, F32), pltpu.SemaphoreType.DMA((solved.shape[0] // GROUP, 4))],
-        compiler_params=pltpu.CompilerParams(vmem_limit_bytes=20 << 20),
+        compiler_params=pltpu.CompilerParams(vmem_limit_bytes=12 << 20),
     )(solved, gains, theirs, mine)
 
 
@@ -308,6 +313,7 @@
         received = swapped(kept, "tile", bit)
         bit *= 2
     solved, gains = freed(highs, lows, inverses)
+    received, solved, gains = lax.optimization_barrier((received, solved, gains))
     mapped = section_map(tiles, received, kept, sep_rhs[0], sep_inverse[0], sep_coupling[0])
     if sections == 4:
         other = swapped(mapped, "chain", 1)

time: 57.3 us -> 37 us (0.65)
  local copies, waits for them, and re-layouts: 17.4 us -> 4.87 us
  Pallas kernels: 14.6 us -> 10.4 us
  waiting for transfers between devices: 16.3 us -> 12.9 us
    unnamed x32 -> x10, local copies, waits for them, and re-layouts: 15.5 us -> 4.21 us
    ppermute x5, waiting for transfers between devices: 16.3 us -> 12.9 us  [swapped(): return lax.ppermute(block, axis, route)]
    slice x2, local copies, waits for them, and re-layouts: 1.31 us -> 0.02 us  [shards(): sep_values = affine(mapped[:, half:], carry, mapped[:, :half])]
    pallas_call x1, Pallas kernels: 1.41 us -> 0.23 us  [section_map(): pl.pallas_call(functools.partial(section_kernel, tiles), out_shape=VMEM(k...]
    pallas_call x1, Pallas kernels: 1.21 us -> 0.19 us  [paired(): pl.pallas_call(pair_kernel, out_shape=VMEM((mine.shape[0], half), F32), i...]
    pallas_call x1, Pallas kernels: 1.18 us -> 0.19 us  [affine(): pl.pallas_call(affine_kernel, out_shape=VMEM(offset.shape, F32), in_specs...]
    pallas_call x1, Pallas kernels: 1.01 us -> 0.02 us  [carried(): pl.pallas_call(carry_kernel, out_shape=VMEM(received.shape, F32), in_spec...]
  transfers between devices with their start and end apart: 5 -> 5, of which waited for: 4 -> 5; matrix products, arithmetic and copies ran while one was open for 3% -> 2% of each run, Pallas kernels for 5% -> 6%
where the time goes in v3:
time: 37 us; the launch traced here: 36.8 us
  waiting for transfers between devices  12.9 us (35%)
  Pallas kernels  10.4 us (28%)
  starting transfers between devices  7.94 us (21%)
  local copies, waits for them, and re-layouts  4.87 us (13%)
  between operations  0.74 us (2%)
    ppermute x5, waiting for transfers between devices, swapped(): return lax.ppermute(block, axis, route)  12.9 us
    ppermute x5, starting transfers between devices, swapped(): return lax.ppermute(block, axis, route)  7.94 us
    pallas_call x1, Pallas kernels, reduced(): pl.pallas_call(functools.partial(reduce_kernel, tiles), out_shape=(VMEM((...  5.37 us
    unnamed x10, local copies, waits for them, and re-layouts  4.21 us
    pallas_call x1, Pallas kernels, leaf_values(): pl.pallas_call(functools.partial(last_kernel, tiles), out_shape=jax.Shape...  2.57 us
    pallas_call x1, Pallas kernels, freed(): pl.pallas_call(free_kernel, out_shape=(VMEM((leaves, rows, columns), F32)...  1.84 us
  transfers between devices with their start and end apart: 5, of which 5 were waited for; matrix products, arithmetic and copies ran while one was open for 2% of the time, Pallas kernels for 6%

profile of v3, /device:TPU:0, one launch (start us, length us, event | category | flops | bytes accessed | tf_op | source)
XLA Modules:
  0.0 36.8 jit_solution(7461842342166516345)
XLA Ops:
  0.6 5.4 %shard_map.95 = (f32[128,384]{1,0:T(8,128)S(1)}, f32[128,384]{1,0:T(8,128)S(1)}, bf16[16,128,640]{2,1,0:T(8,128)(2,1)S(1)}, bf16[16,128,640]{2,1,0:T(8,128)(2,1)S(1)}, bf16[16,128,384]{2,1,0:T(8,128)(2,1)S(1)}) custom-call(s32[1,16]{1,0:T(1,128)} %pattern.1, f32[16,128,512]{2,1,0:T(8,128)} %bitcast.13, f32[16,128,128]{2,1,0:T(8,128)} %bitcast.15, ...), custom_call_target="tpu_custom_call" | custom-call | tf_op jit(solution)/shard_map/pallas_call | solution.py:113
  6.0 0.5 %collective-permute-start = (f32[128,384]{1,0:T(8,128)S(1)}, f32[128,384]{1,0:T(8,128)S(1)}, u32[]{:S(2)}, u32[]{:S(2)}) collective-permute-start(f32[128,384]{1,0:T(8,128)S(1)} %get-tuple-element.13), channel_id=1, source_target_pairs={{0,1},{1,0},{2,3},{3,2},{4,5},{5,4},{6,7},{7,6},{8,9},{9,8},{10,11... | collective-permute-start | bytes 589832 | tf_op jit(solution)/shard_map/ppermute | solution.py:22
  6.5 1.1 %collective-permute-done = f32[128,384]{1,0:T(8,128)S(1)} collective-permute-done((f32[128,384]{1,0:T(8,128)S(1)}, f32[128,384]{1,0:T(8,128)S(1)}, u32[]{:S(2)}, u32[]{:S(2)}) %collective-permute-start) | collective-permute-done | bytes 196640 | tf_op jit(solution)/shard_map/ppermute | solution.py:22
  7.6 3.0 %collective-permute-start.1 = (f32[128,384]{1,0:T(8,128)S(1)}, f32[128,384]{1,0:T(8,128)S(1)}, u32[]{:S(2)}, u32[]{:S(2)}) collective-permute-start(f32[128,384]{1,0:T(8,128)S(1)} %add.7.kept), channel_id=1, source_target_pairs={{0,2},{1,3},{2,0},{3,1},{4,6},{5,7},{6,4},{7,5},{8,10},{9,11},{10,... | collective-permute-start | bytes 589832 | tf_op jit(solution)/shard_map/ppermute | solution.py:22
  10.6 0.0 copy-start.2
  10.6 1.8 %shard_map.96 = (f32[16,128,512]{2,1,0:T(8,128)S(1)}, bf16[16,128,384]{2,1,0:T(8,128)(2,1)S(1)}) custom-call(bf16[16,128,640]{2,1,0:T(8,128)(2,1)S(1)} %get-tuple-element.14.highs, bf16[16,128,640]{2,1,0:T(8,128)(2,1)S(1)} %get-tuple-element.15.lows, bf16[16,128,384]{2,1,0:T(8,128)(2,1)S(1)} %get-tuple-element.16.inverses), custom_call_target="tpu_custom_call" | custom-call | flops 1006632960 | bytes 10485760 | tf_op jit(solution)/shard_map/pallas_call | solution.py:146
  12.4 0.0 copy-start
  12.4 2.0 %copy-done = f32[16,128,512]{2,1,0:T(8,128)} copy-done((f32[16,128,512]{2,1,0:T(8,128)}, f32[16,128,512]{2,1,0:T(8,128)S(1)}, u32[]{:S(2)}) %copy-start) | copy-done | bytes 4194328
  14.4 1.3 %collective-permute-done.1.received = f32[128,384]{1,0:T(8,128)S(1)} collective-permute-done((f32[128,384]{1,0:T(8,128)S(1)}, f32[128,384]{1,0:T(8,128)S(1)}, u32[]{:S(2)}, u32[]{:S(2)}) %collective-permute-start.1) | collective-permute-done | bytes 196640 | tf_op jit(solution)/shard_map/ppermute | solution.py:22
  15.8 0.0 copy-done.2
  15.8 0.0 copy-done.3
  15.8 0.0 copy-done.4
  15.8 0.2 shard_map.97.mine
  16.0 1.9 %collective-permute-start.2 = (f32[128,384]{1,0:T(8,128)S(1)}, f32[128,384]{1,0:T(8,128)S(1)}, u32[]{:S(2)}, u32[]{:S(2)}) collective-permute-start(f32[128,384]{1,0:T(8,128)S(1)} %shard_map.97.mine), channel_id=1, source_target_pairs={{0,4},{4,0},{8,12},{12,8},{1,5},{5,1},{9,13},{13,9},{2,6},{6,2},{1... | collective-permute-start | bytes 589832 | tf_op jit(solution)/shard_map/ppermute | solution.py:22
  17.9 4.6 %collective-permute-done.2.other = f32[128,384]{1,0:T(8,128)S(1)} collective-permute-done((f32[128,384]{1,0:T(8,128)S(1)}, f32[128,384]{1,0:T(8,128)S(1)}, u32[]{:S(2)}, u32[]{:S(2)}) %collective-permute-start.2) | collective-permute-done | bytes 196640 | tf_op jit(solution)/shard_map/ppermute | solution.py:22
  22.5 0.2 shard_map.98
  22.7 2.5 %collective-permute-start.3 = (f32[128,256]{1,0:T(8,128)S(1)}, f32[128,256]{1,0:T(8,128)S(1)}, u32[]{:S(2)}, u32[]{:S(2)}) collective-permute-start(f32[128,256]{1,0:T(8,128)S(1)} %shard_map.98), channel_id=1, source_target_pairs={{0,8},{4,12},{8,0},{12,4},{1,9},{5,13},{9,1},{13,5},{2,10},{6,14},... | collective-permute-start | bytes 393224 | tf_op jit(solution)/shard_map/ppermute | solution.py:22
  25.3 5.4 %collective-permute-done.3.received = f32[128,256]{1,0:T(8,128)S(1)} collective-permute-done((f32[128,256]{1,0:T(8,128)S(1)}, f32[128,256]{1,0:T(8,128)S(1)}, u32[]{:S(2)}, u32[]{:S(2)}) %collective-permute-start.3) | collective-permute-done | bytes 131104 | tf_op jit(solution)/shard_map/ppermute | solution.py:22
  30.7 0.1 collective-permute-start.4
  30.8 0.2 shard_map.101
  31.0 0.6 %dynamic-slice_bitcast_fusion = f32[1,128,128]{2,1,0:T(8,128)} fusion(f32[128,256]{1,0:T(8,128)S(1)} %shard_map.101, s32[]{:T(128)S(6)} %select_n.9), kind=kLoop, calls=%fused_computation | loop fusion | bytes 131076 | tf_op jit(solution)/shard_map/broadcast_in_dim | solution.py:333
  31.6 0.4 %collective-permute-done.4.theirs = f32[128,256]{1,0:T(8,128)S(1)} collective-permute-done((f32[128,256]{1,0:T(8,128)S(1)}, f32[128,256]{1,0:T(8,128)S(1)}, u32[]{:S(2)}, u32[]{:S(2)}) %collective-permute-start.4) | collective-permute-done | bytes 131104 | tf_op jit(solution)/shard_map/ppermute | solution.py:22
  32.1 2.2 %copy-done.1 = f32[16,128,512]{2,1,0:T(8,128)S(1)} copy-done((f32[16,128,512]{2,1,0:T(8,128)S(1)}, f32[16,128,512]{2,1,0:T(8,128)}, u32[]{:S(2)}) %copy-start.1) | copy-done | bytes 4194328
  34.3 2.6 %shard_map.100 = f32[16,128,512]{2,1,0:T(8,128)} custom-call(f32[16,128,512]{2,1,0:T(8,128)S(1)} %copy-done.1, bf16[16,128,384]{2,1,0:T(8,128)(2,1)S(1)} %get-tuple-element.20.gains, f32[128,256]{1,0:T(8,128)S(1)} %collective-permute-done.4.theirs, f32[128,256]{1,0:T(8,128)S(1)} %shard_map.99.mine.block), custom_call_target="tpu_custom_call" | custom-call | tf_op jit(solution)/shard_map/pallas_call | solution.py:279
  (7 shorter events, 0.1 us)
Async XLA Ops:
  6.0 1.6 %collective-permute-start = (f32[128,384]{1,0:T(8,128)S(1)}, f32[128,384]{1,0:T(8,128)S(1)}, u32[]{:S(2)}, u32[]{:S(2)}) collective-permute-start(f32[128,384]{1,0:T(8,128)S(1)} %get-tuple-element.13), channel_id=1, source_target_pairs={{0,1},{1,0},{2,3},{3,2},{4,5},{5,4},{6,7},{7,6},{8,9},{9,8},{10,11... | collective-permute-start | bytes 589832 | tf_op jit(solution)/shard_map/ppermute | solution.py:22
  7.6 8.2 %collective-permute-start.1 = (f32[128,384]{1,0:T(8,128)S(1)}, f32[128,384]{1,0:T(8,128)S(1)}, u32[]{:S(2)}, u32[]{:S(2)}) collective-permute-start(f32[128,384]{1,0:T(8,128)S(1)} %add.7.kept), channel_id=1, source_target_pairs={{0,2},{1,3},{2,0},{3,1},{4,6},{5,7},{6,4},{7,5},{8,10},{9,11},{10,... | collective-permute-start | bytes 589832 | tf_op jit(solution)/shard_map/ppermute | solution.py:22
  10.6 5.2 %copy-start.2 = (f32[1,128,512]{2,1,0:T(8,128)S(1)}, f32[1,128,512]{2,1,0:T(8,128)}, u32[]{:S(2)}) copy-start(f32[1,128,512]{2,1,0:T(8,128)} %param.13) | copy-start | bytes 786436
  10.6 5.2 %copy-start.3 = (f32[1,128,128]{2,1,0:T(8,128)S(1)}, f32[1,128,128]{2,1,0:T(8,128)}, u32[]{:S(2)}) copy-start(f32[1,128,128]{2,1,0:T(8,128)} %param.14) | copy-start | bytes 196612
  10.6 5.2 %copy-start.4 = (f32[1,128,128]{2,1,0:T(8,128)S(1)}, f32[1,128,128]{2,1,0:T(8,128)}, u32[]{:S(2)}) copy-start(f32[1,128,128]{2,1,0:T(8,128)} %param.15) | copy-start | bytes 196612
  12.4 2.0 %copy-start = (f32[16,128,512]{2,1,0:T(8,128)}, f32[16,128,512]{2,1,0:T(8,128)S(1)}, u32[]{:S(2)}) copy-start(f32[16,128,512]{2,1,0:T(8,128)S(1)} %get-tuple-element.19.solved) | copy-start | bytes 12582916
  16.0 6.5 %collective-permute-start.2 = (f32[128,384]{1,0:T(8,128)S(1)}, f32[128,384]{1,0:T(8,128)S(1)}, u32[]{:S(2)}, u32[]{:S(2)}) collective-permute-start(f32[128,384]{1,0:T(8,128)S(1)} %shard_map.97.mine), channel_id=1, source_target_pairs={{0,4},{4,0},{8,12},{12,8},{1,5},{5,1},{9,13},{13,9},{2,6},{6,2},{1... | collective-permute-start | bytes 589832 | tf_op jit(solution)/shard_map/ppermute | solution.py:22
  22.7 7.9 %collective-permute-start.3 = (f32[128,256]{1,0:T(8,128)S(1)}, f32[128,256]{1,0:T(8,128)S(1)}, u32[]{:S(2)}, u32[]{:S(2)}) collective-permute-start(f32[128,256]{1,0:T(8,128)S(1)} %shard_map.98), channel_id=1, source_target_pairs={{0,8},{4,12},{8,0},{12,4},{1,9},{5,13},{9,1},{13,5},{2,10},{6,14},... | collective-permute-start | bytes 393224 | tf_op jit(solution)/shard_map/ppermute | solution.py:22
  30.7 1.4 %collective-permute-start.4 = (f32[128,256]{1,0:T(8,128)S(1)}, f32[128,256]{1,0:T(8,128)S(1)}, u32[]{:S(2)}, u32[]{:S(2)}) collective-permute-start(f32[128,256]{1,0:T(8,128)S(1)} %shard_map.99.mine.block), channel_id=1, source_target_pairs={{0,1},{1,0},{2,3},{3,2},{4,5},{5,4},{6,7},{7,6},{8,9},{9,8},{10,11... | collective-permute-start | bytes 393224 | tf_op jit(solution)/shard_map/ppermute | solution.py:22
  32.1 2.2 %copy-start.1 = (f32[16,128,512]{2,1,0:T(8,128)S(1)}, f32[16,128,512]{2,1,0:T(8,128)}, u32[]{:S(2)}) copy-start(f32[16,128,512]{2,1,0:T(8,128)} %copy-done) | copy-start | bytes 12582916

commit v4 on v2

v4 whole, which is shorter than its diff:
```python
import functools

import jax
import jax.numpy as jnp
from jax import lax
from jax.experimental import pallas as pl
from jax.experimental.pallas import tpu as pltpu
from jax.sharding import PartitionSpec as P

F32 = jnp.float32
BF16 = jnp.bfloat16
LANES = 128
VMEM = pltpu.MemorySpace.VMEM
IN_VMEM = pl.BlockSpec(memory_space=pltpu.VMEM)
IN_HBM = pl.BlockSpec(memory_space=pl.ANY)
GROUP = 4
SMALL = 4 << 20


def swapped(block, axis, bit):
    route = [(i, i ^ bit) for i in range(lax.axis_size(axis))]
    return lax.ppermute(block, axis, route)


def parts_of(block):
    high = block.astype(BF16)
    return high, (block - high.astype(F32)).astype(BF16)


def matmul(left, right):
    return lax.dot_general(left, right, (((1,), (0,)), ((), ())), preferred_element_type=F32)


def left_of(block):
    high, low = parts_of(block)
    return jnp.concatenate([high, low, high], 1)


def right_of(block):
    high, low = parts_of(block)
    return jnp.concatenate([high, high, low], 0)


def product(left, right):
    return matmul(left_of(left), right_of(right))


def starts(tiles, which):
    if tiles == 4:
        return [which * LANES, which * LANES + 2 * LANES]
    return [which * 2 * LANES, which * 2 * LANES + LANES]


def lanes(start):
    return pl.ds(pl.multiple_of(start, LANES), LANES)


def reduce_kernel(tiles, pattern, rhs, inverse, coupling, update, sent_a, kept_a, sent_b, kept_b, highs, lows, inverses, right, tiles_a, tiles_b, sems):
    leaves = rhs.shape[0]
    core = lax.rem(lax.axis_index("tile"), 2)
    other, own = starts(tiles, 1 - core), starts(tiles, core)
    order = [other[0], own[0], other[1], own[1]]
    copies = []
    for k in range(leaves // GROUP):
        some = pl.ds(k * GROUP, GROUP)
        pair = [
            pltpu.make_async_copy(update.at[some], tiles_a.at[some], sems.at[k, 0]),
            pltpu.make_async_copy(inverse.at[some], tiles_b.at[some], sems.at[k, 1]),
        ]
        for copy in pair:
            copy.start()
        copies.append(pair)
    blocks = []
    for k in range(leaves // GROUP):
        some = pl.ds(k * GROUP, GROUP)
        row = [pltpu.make_async_copy(coupling.at[some], right.at[some, :, pl.ds(0, LANES)], sems.at[k, 6])]
        for j, start in enumerate(order):
            row.append(pltpu.make_async_copy(rhs.at[some, :, lanes(start)], right.at[some, :, pl.ds((j + 1) * LANES, LANES)], sems.at[k, 2 + j]))
        for copy in row:
            copy.start()
        blocks.append(row)
    lefts = []
    for k in range(leaves // GROUP):
        for copy in copies[k]:
            copy.wait()
        for leaf in range(k * GROUP, k * GROUP + GROUP):
            inv_high, inv_low = parts_of(tiles_b[leaf])
            inverses[leaf] = jnp.concatenate([inv_high, inv_low, inv_high], 1)
            masked = tiles_a[leaf] * pattern[0, leaf].astype(F32)
            lefts.append(left_of(matmul(left_of(masked), jnp.concatenate([inv_high, inv_high, inv_low], 0))))
    total = None
    for k in range(leaves // GROUP):
        for copy in blocks[k]:
            copy.wait()
        stacked = []
        for leaf in range(k * GROUP, k * GROUP + GROUP):
            high, low = parts_of(right[leaf])
            highs[leaf] = high
            lows[leaf] = low
            stacked += [high, high, low]
        here = matmul(jnp.concatenate(lefts[k * GROUP : k * GROUP + GROUP], 1), jnp.concatenate(stacked, 0))
        total = here if total is None else total + here
    cross, other_a, own_a, other_b, own_b = [total[:, j * LANES : (j + 1) * LANES] for j in range(5)]
    sent_a[...] = jnp.concatenate([cross, other_a], 1)
    kept_a[...] = jnp.concatenate([cross, own_a], 1)
    sent_b[...] = other_b
    kept_b[...] = own_b


def reduced(tiles, pattern, rhs, inverse, coupling, update):
    leaves, rows, columns = rhs.shape
    wide = columns + rows
    return pl.pallas_call(
        functools.partial(reduce_kernel, tiles),
        out_shape=(
            VMEM((rows, 2 * LANES), F32),
            VMEM((rows, 2 * LANES), F32),
            VMEM((rows, LANES), F32),
            VMEM((rows, LANES), F32),
            VMEM((leaves, rows, wide), BF16),
            VMEM((leaves, rows, wide), BF16),
            VMEM((leaves, rows, 3 * rows), BF16),
        ),
        in_specs=[pl.BlockSpec(memory_space=pltpu.SMEM)] + [IN_HBM] * 4,
        out_specs=(IN_VMEM,) * 7,
        scratch_shapes=[
            pltpu.VMEM((leaves, rows, wide), F32),
            pltpu.VMEM((leaves, rows, rows), F32),
            pltpu.VMEM((leaves, rows, rows), F32),
            pltpu.SemaphoreType.DMA((leaves // GROUP, 7)),
        ],
        compiler_params=pltpu.CompilerParams(vmem_limit_bytes=50 << 20),
    )(pattern, rhs, inverse, coupling, update)


def free_kernel(highs, lows, inverses, solved_a, solved_b, gains):
    for leaf in range(highs.shape[0]):
        high = highs[leaf]
        here = matmul(inverses[leaf], jnp.concatenate([high, high, lows[leaf]], 0))
        gains[leaf] = left_of(here[:, :LANES])
        solved_a[leaf] = here[:, LANES : 3 * LANES]
        solved_b[leaf] = here[:, 3 * LANES :]


def freed(highs, lows, inverses):
    leaves, rows, wide = highs.shape
    return pl.pallas_call(
        free_kernel,
        out_shape=(VMEM((leaves, rows, 2 * LANES), F32), VMEM((leaves, rows, 2 * LANES), F32), VMEM((leaves, rows, 3 * rows), BF16)),
        in_specs=[IN_VMEM] * 3,
        out_specs=(IN_VMEM,) * 3,
        compiler_params=pltpu.CompilerParams(vmem_limit_bytes=8 << 20),
        cost_estimate=pl.CostEstimate(flops=6 * leaves * rows * rows * wide, bytes_accessed=leaves * rows * wide * 8, transcendentals=0),
    )(highs, lows, inverses)


def small(kernel, out_shape, *operands):
    return pl.pallas_call(
        kernel,
        out_shape=out_shape,
        in_specs=[IN_VMEM] * len(operands),
        out_specs=jax.tree.map(lambda _: IN_VMEM, out_shape),
        compiler_params=pltpu.CompilerParams(vmem_limit_bytes=SMALL),
    )(*operands)


def map_kernel(tiles, received, kept, sep_rhs, sep_inverse, sep_coupling, mapped):
    start = starts(tiles, lax.rem(lax.axis_index("tile"), 2))[0]
    right = jnp.concatenate([sep_coupling[...], sep_rhs[:, lanes(start)]], 1)
    mapped[...] = product(sep_inverse[...], right - (received[...] + kept[...]))


def offset_kernel(tiles, received, kept, sep_rhs, sep_inverse, after, offset):
    start = starts(tiles, lax.rem(lax.axis_index("tile"), 2))[1]
    offset[...] = product(sep_inverse[...], sep_rhs[:, lanes(start)] - (received[...] + kept[...]))


def pair_kernel(mine_step, mine, other_step, other, after, whole):
    @pl.when(lax.rem(lax.axis_index("chain"), 2) == 1)
    def _():
        whole[...] = mine[...] - product(mine_step[...], other[...])

    @pl.when(lax.rem(lax.axis_index("chain"), 2) == 0)
    def _():
        whole[...] = other[...] - product(other_step[...], mine[...])


def carry_kernel(other_step, other, received, after, carry):
    section = lax.axis_index("chain")

    @pl.when(section == 0)
    def _():
        carry[...] = jnp.zeros_like(carry)

    @pl.when(section == 1)
    def _():
        carry[...] = other[...]

    @pl.when(section == 2)
    def _():
        carry[...] = received[...]

    @pl.when(section == 3)
    def _():
        carry[...] = other[...] - product(other_step[...], received[...])


def affine_kernel(step, block, offset, result):
    result[...] = offset[...] - product(step[...], block[...])


def affine(step, block, offset):
    return small(affine_kernel, VMEM(offset.shape, F32), step, block, offset)


def scanned(section, solved, half):
    sections = lax.axis_size("chain")
    whole_b, whole_a = solved[:, :half], solved[:, half:]
    before_b, before_a = jnp.zeros_like(whole_b), -jnp.eye(whole_a.shape[0], dtype=F32)
    nothing = jnp.zeros_like(whole_a)
    bit = 1
    while bit < sections:
        upper = (section // bit) % 2 == 1
        other = swapped(jnp.concatenate([whole_b, whole_a], 1), "chain", bit)
        other_b, other_a = other[:, :half], other[:, half:]
        before_b = jnp.where(upper, affine(before_a, other_b, before_b), before_b)
        before_a = jnp.where(upper, affine(before_a, other_a, nothing), before_a)
        first_b, first_a = jnp.where(upper, other_b, whole_b), jnp.where(upper, other_a, whole_a)
        second_b, second_a = jnp.where(upper, whole_b, other_b), jnp.where(upper, whole_a, other_a)
        whole_b = affine(second_a, first_b, second_b)
        whole_a = affine(second_a, first_a, nothing)
        bit *= 2
    return before_b


def last_kernel(tiles, chunk, solved, gains, theirs, mine, *refs):
    leaves = solved.shape[0]
    core = lax.rem(lax.axis_index("tile"), 2)
    order = [starts(tiles, 1 - core)[chunk], starts(tiles, core)[chunk]]
    copies = []
    if len(refs) > 4:
        step, offset_a, carry_a, offset_b, _, out, share_out, values, share, sems, share_sem = refs
        first = lax.axis_index("tile") < 2
        here = product(step[...], jnp.where(first, carry_a[...], mine[...]))
        share[...] = jnp.where(first, offset_a[...], offset_b[...]) - here
        copies.append(pltpu.make_async_copy(share, share_out, share_sem))
        copies[0].start()
    else:
        out, values, sems = refs[-3:]
    right = jnp.concatenate([right_of(theirs[...]), right_of(mine[...])], 1)
    for k in range(leaves // GROUP):
        for leaf in range(k * GROUP, k * GROUP + GROUP):
            values[leaf] = solved[leaf] - matmul(gains[leaf], right)
        some = pl.ds(k * GROUP, GROUP)
        for j, start in enumerate(order):
            copy = pltpu.make_async_copy(values.at[some, :, pl.ds(j * LANES, LANES)], out.at[some, :, lanes(start)], sems.at[k, j])
            copy.start()
            copies.append(copy)
    for copy in copies:
        copy.wait()


def leaf_values(tiles, chunk, solved, gains, theirs, mine, shared, *before):
    leaves, rows, width = solved.shape
    out_shape = [jax.ShapeDtypeStruct((leaves, rows, 2 * width), F32)]
    scratch = [pltpu.VMEM(solved.shape, F32)]
    sems = [pltpu.SemaphoreType.DMA((leaves // GROUP, 2))]
    if shared:
        out_shape.append(jax.ShapeDtypeStruct((rows, LANES), F32))
        scratch.append(pltpu.VMEM((rows, LANES), F32))
        sems.append(pltpu.SemaphoreType.DMA)
    return pl.pallas_call(
        functools.partial(last_kernel, tiles, chunk),
        out_shape=out_shape,
        in_specs=[IN_VMEM] * (4 + len(shared)) + [IN_HBM] * len(before),
        out_specs=[IN_HBM] * len(out_shape),
        scratch_shapes=scratch + sems,
        input_output_aliases={4 + len(shared): 0} if before else {},
        compiler_params=pltpu.CompilerParams(vmem_limit_bytes=8 << 20),
        cost_estimate=pl.CostEstimate(flops=6 * leaves * rows * rows * width, bytes_accessed=leaves * rows * width * 8, transcendentals=0),
    )(solved, gains, theirs, mine, *shared, *before)


def shards(
    leaf_rhs,
    leaf_inverse,
    leaf_coupling,
    leaf_update,
    update_pattern,
    sep_rhs,
    sep_inverse,
    sep_coupling,
):
    tiles = lax.axis_size("tile")
    sections = lax.axis_size("chain")
    tile = lax.axis_index("tile")
    section = lax.axis_index("chain")
    columns = sep_rhs.shape[2]
    width = columns // tiles
    block = VMEM((sep_rhs.shape[1], LANES), F32)
    double = VMEM((sep_rhs.shape[1], 2 * LANES), F32)

    sent_a, kept_a, sent_b, kept_b, highs, lows, inverses = reduced(
        tiles, update_pattern, leaf_rhs[0], leaf_inverse[0], leaf_coupling[0], leaf_update[0]
    )
    kept_a = kept_a + swapped(sent_a, "tile", 1)
    kept_b = kept_b + swapped(sent_b, "tile", 1)
    received_a = swapped(kept_a, "tile", 2) if tiles > 2 else jnp.zeros_like(kept_a)
    received_b = swapped(kept_b, "tile", 2) if tiles > 2 else jnp.zeros_like(kept_b)
    bit = 4
    while bit < tiles:
        kept_a, kept_b = kept_a + received_a, kept_b + received_b
        received_a, received_b = swapped(kept_a, "tile", bit), swapped(kept_b, "tile", bit)
        bit *= 2
    solved_a, solved_b, gains = freed(highs, lows, inverses)
    received_a, solved_a, solved_b, gains = lax.optimization_barrier((received_a, solved_a, solved_b, gains))
    mapped = small(functools.partial(map_kernel, tiles), double, received_a, kept_a, sep_rhs[0], sep_inverse[0], sep_coupling[0])
    offset_b = small(functools.partial(offset_kernel, tiles), block, received_b, kept_b, sep_rhs[0], sep_inverse[0], mapped)
    step, offset_a = mapped[:, :LANES], mapped[:, LANES:]
    if sections == 4:
        other = swapped(mapped, "chain", 1)
        other_step, other_a = other[:, :LANES], other[:, LANES:]
        other_b = swapped(offset_b, "chain", 1)
        whole_a = small(pair_kernel, block, step, offset_a, other_step, other_a, offset_b)
        met_a = swapped(whole_a, "chain", 2)
        whole_b = small(pair_kernel, block, step, offset_b, other_step, other_b, whole_a)
        met_b = swapped(whole_b, "chain", 2)
        carry_a = small(carry_kernel, block, other_step, other_a, met_a, whole_b)
        carry_b = small(carry_kernel, block, other_step, other_b, met_b, carry_a)
    else:
        carry = scanned(section, jnp.concatenate([offset_a, offset_b, step], 1), 2 * LANES)
        carry_a, carry_b = carry[:, :LANES], carry[:, LANES:]
    theirs_a = swapped(carry_a, "tile", 1)
    (leaf_share,) = leaf_values(tiles, 0, solved_a, gains, theirs_a, carry_a, ())
    theirs_b = swapped(carry_b, "tile", 1)
    if tiles == 4:
        shared = (step, offset_a, carry_a, offset_b)
        leaf_share, sep_share = leaf_values(tiles, 1, solved_b, gains, theirs_b, carry_b, shared, leaf_share)
    else:
        (leaf_share,) = leaf_values(tiles, 1, solved_b, gains, theirs_b, carry_b, (), leaf_share)
        own = affine(step, jnp.concatenate([carry_a, carry_b], 1), jnp.concatenate([offset_a, offset_b], 1))
        others = swapped(own, "tile", 1)
        lower = jnp.where(tile % 2 == 0, own, others)
        upper = jnp.where(tile % 2 == 0, others, own)
        sep_share = lax.dynamic_slice_in_dim(jnp.concatenate([lower, upper], 1), tile * width, width, 1)
    return (leaf_share[None], sep_share[None])


def solution(mesh):
    return jax.shard_map(
        shards,
        mesh=mesh,
        in_specs=(
            P(("parts", "chain"), "tile", None, None),
            P(("parts", "chain"), "tile", None, None),
            P(("parts", "chain"), "tile", None, None),
            P(("parts", "chain"), "tile", None, None),
            P(("parts", "chain"), "tile"),
            P(("parts", "chain"), None, None),
            P(("parts", "chain"), None, None),
            P(("parts", "chain"), None, None),
        ),
        out_specs=(P(("parts", "chain"), "tile", None, None), P(("parts", "chain"), None, "tile")),
        check_vma=False,
    )
```

time: 57.3 us -> 32.4 us (0.57)
  local copies, waits for them, and re-layouts: 17.4 us -> 0.03 us
  waiting for transfers between devices: 16.3 us -> 9.67 us
  Pallas kernels: 14.6 us -> 11.4 us
  starting transfers between devices: 7.87 us -> 10.4 us
    unnamed x32 -> x6, local copies, waits for them, and re-layouts: 15.5 us -> 0.01 us
    ppermute x5 -> x10, waiting for transfers between devices: 16.3 us -> 9.67 us  [swapped(): return lax.ppermute(block, axis, route)]
    pallas_call x6 -> x9, Pallas kernels: 9.19 us -> 5.98 us  [the longest x2 3.42 us: leaf_values(): pl.pallas_call(functools.partial(last_kernel, tiles, chunk), out_shape=ou...]
    ppermute x5 -> x10, starting transfers between devices: 7.87 us -> 10.4 us  [swapped(): return lax.ppermute(block, axis, route)]
    slice x2, local copies, waits for them, and re-layouts: 1.31 us -> 0.02 us  [the longest x1 0.01 us: shards(): step, offset_a = (mapped[:, :LANES], mapped[:, LANES:])]
    broadcast_in_dim x1 -> x0, local copies, waits for them, and re-layouts: 0.64 us -> none  [shards(): sep_share[None]]
  transfers between devices with their start and end apart: 5 -> 10, of which waited for: 4 -> 5; matrix products, arithmetic and copies ran while one was open for 3% -> 0% of each run, Pallas kernels for 5% -> 13%
where the time goes in v4:
time: 32.4 us; the launch traced here: 32.2 us
  Pallas kernels  11.4 us (35%)
  starting transfers between devices  10.4 us (32%)
  waiting for transfers between devices  9.67 us (30%)
  between operations  0.75 us (2%)
    ppermute x10, starting transfers between devices, swapped(): return lax.ppermute(block, axis, route)  10.4 us
    ppermute x10, waiting for transfers between devices, swapped(): return lax.ppermute(block, axis, route)  9.67 us
    pallas_call x1, Pallas kernels, reduced(): pl.pallas_call(functools.partial(reduce_kernel, tiles), out_shape=(VMEM((...  5.37 us
    pallas_call x2, Pallas kernels, leaf_values(): pl.pallas_call(functools.partial(last_kernel, tiles, chunk), out_shape=ou...  3.42 us
    pallas_call x1, Pallas kernels, freed(): pl.pallas_call(free_kernel, out_shape=(VMEM((leaves, rows, 2 * LANES), F3...  1.81 us
    pallas_call x6, Pallas kernels, small(): pl.pallas_call(kernel, out_shape=out_shape, in_specs=[IN_VMEM] * len(oper...  0.75 us
  transfers between devices with their start and end apart: 10, of which 5 were waited for; matrix products, arithmetic and copies ran while one was open for 0% of the time, Pallas kernels for 13%

profile of v4, /device:TPU:0, one launch (start us, length us, event | category | flops | bytes accessed | tf_op | source)
XLA Modules:
  0.0 32.2 jit_solution(5948314006041701962)
XLA Ops:
  0.6 5.4 %shard_map.95 = (f32[128,256]{1,0:T(8,128)S(1)}, f32[128,256]{1,0:T(8,128)S(1)}, f32[128,128]{1,0:T(8,128)S(1)}, f32[128,128]{1,0:T(8,128)S(1)}, bf16[16,128,640...) custom-call(s32[1,16]{1,0:T(1,128)} %pattern.1, ...), custom_call_target="tpu_custom_call" | custom-call | tf_op jit(solution)/shard_map/pallas_call | solution.py:113
  6.0 0.5 %collective-permute-start = (f32[128,256]{1,0:T(8,128)S(1)}, f32[128,256]{1,0:T(8,128)S(1)}, u32[]{:S(2)}, u32[]{:S(2)}) collective-permute-start(f32[128,256]{1,0:T(8,128)S(1)} %get-tuple-element.19), channel_id=1, source_target_pairs={{0,1},{1,0},{2,3},{3,2},{4,5},{5,4},{6,7},{7,6},{8,9},{9,8},{10,11... | collective-permute-start | bytes 393224 | tf_op jit(solution)/shard_map/ppermute | solution.py:22
  6.5 0.1 collective-permute-start.3
  6.6 0.9 %collective-permute-done = f32[128,256]{1,0:T(8,128)S(1)} collective-permute-done((f32[128,256]{1,0:T(8,128)S(1)}, f32[128,256]{1,0:T(8,128)S(1)}, u32[]{:S(2)}, u32[]{:S(2)}) %collective-permute-start) | collective-permute-done | bytes 131104 | tf_op jit(solution)/shard_map/ppermute | solution.py:22
  7.5 2.9 %collective-permute-start.1 = (f32[128,256]{1,0:T(8,128)S(1)}, f32[128,256]{1,0:T(8,128)S(1)}, u32[]{:S(2)}, u32[]{:S(2)}) collective-permute-start(f32[128,256]{1,0:T(8,128)S(1)} %add.6.kept), channel_id=1, source_target_pairs={{0,2},{1,3},{2,0},{3,1},{4,6},{5,7},{6,4},{7,5},{8,10},{9,11},{10,... | collective-permute-start | bytes 393224 | tf_op jit(solution)/shard_map/ppermute | solution.py:22
  10.5 0.1 collective-permute-start.4
  10.6 0.0 copy-start.2
  10.6 1.8 %shard_map.96 = (f32[16,128,256]{2,1,0:T(8,128)S(1)}, f32[16,128,256]{2,1,0:T(8,128)S(1)}, bf16[16,128,384]{2,1,0:T(8,128)(2,1)S(1)}) custom-call(bf16[16,128,640]{2,1,0:T(8,128)(2,1)S(1)} %get-tuple-element.20.highs, bf16[16,128,640]{2,1,0:T(8,128)(2,1)S(1)} %get-tuple-element.21.lows, bf16[16,128,384]{2,1,0:T(8,128)(2,1)S(1)} %get-tuple-element.22.inverses), custom_call_target="tpu_custom_call" | custom-call | flops 1006632960 | bytes 10485760 | tf_op jit(solution)/shard_map/pallas_call | solution.py:147
  12.4 2.3 %collective-permute-done.1.received = f32[128,256]{1,0:T(8,128)S(1)} collective-permute-done((f32[128,256]{1,0:T(8,128)S(1)}, f32[128,256]{1,0:T(8,128)S(1)}, u32[]{:S(2)}, u32[]{:S(2)}) %collective-permute-start.1) | collective-permute-done | bytes 131104 | tf_op jit(solution)/shard_map/ppermute | solution.py:22
  14.8 0.2 shard_map.97.after
  15.0 2.1 %collective-permute-start.2 = (f32[128,256]{1,0:T(8,128)S(1)}, f32[128,256]{1,0:T(8,128)S(1)}, u32[]{:S(2)}, u32[]{:S(2)}) collective-permute-start(f32[128,256]{1,0:T(8,128)S(1)} %shard_map.97.after), channel_id=1, source_target_pairs={{0,4},{4,0},{8,12},{12,8},{1,5},{5,1},{9,13},{13,9},{2,6},{6,2},{1... | collective-permute-start | bytes 393224 | tf_op jit(solution)/shard_map/ppermute | solution.py:22
  17.1 0.2 shard_map.98.after.mine.refs_3_
  17.3 0.5 %collective-permute-start.5 = (f32[128,128]{1,0:T(8,128)S(1)}, f32[128,128]{1,0:T(8,128)S(1)}, u32[]{:S(2)}, u32[]{:S(2)}) collective-permute-start(f32[128,128]{1,0:T(8,128)S(1)} %shard_map.98.after.mine.refs_3_), channel_id=1, source_target_pairs={{0,4},{4,0},{8,12},{12,8},{1,5},{5,1},{9,13},{13,9},{2,6},{6,2},{1... | collective-permute-start | bytes 196616 | tf_op jit(solution)/shard_map/ppermute | solution.py:22
  17.7 2.6 %collective-permute-done.2 = f32[128,256]{1,0:T(8,128)S(1)} collective-permute-done((f32[128,256]{1,0:T(8,128)S(1)}, f32[128,256]{1,0:T(8,128)S(1)}, u32[]{:S(2)}, u32[]{:S(2)}) %collective-permute-start.2) | collective-permute-done | bytes 131104 | tf_op jit(solution)/shard_map/ppermute | solution.py:22
  20.4 0.2 shard_map.99.after
  20.6 2.8 %collective-permute-start.7 = (f32[128,128]{1,0:T(8,128)S(1)}, f32[128,128]{1,0:T(8,128)S(1)}, u32[]{:S(2)}, u32[]{:S(2)}) collective-permute-start(f32[128,128]{1,0:T(8,128)S(1)} %shard_map.99.after), channel_id=1, source_target_pairs={{0,8},{4,12},{8,0},{12,4},{1,9},{5,13},{9,1},{13,5},{2,10},{6,14},... | collective-permute-start | bytes 196616 | tf_op jit(solution)/shard_map/ppermute | solution.py:22
  23.3 0.2 shard_map.100.after
  23.5 1.4 %collective-permute-start.6 = (f32[128,128]{1,0:T(8,128)S(1)}, f32[128,128]{1,0:T(8,128)S(1)}, u32[]{:S(2)}, u32[]{:S(2)}) collective-permute-start(f32[128,128]{1,0:T(8,128)S(1)} %shard_map.100.after), channel_id=1, source_target_pairs={{0,8},{4,12},{8,0},{12,4},{1,9},{5,13},{9,1},{13,5},{2,10},{6,14},... | collective-permute-start | bytes 196616 | tf_op jit(solution)/shard_map/ppermute | solution.py:22
  24.9 2.3 %collective-permute-done.7.received = f32[128,128]{1,0:T(8,128)S(1)} collective-permute-done((f32[128,128]{1,0:T(8,128)S(1)}, f32[128,128]{1,0:T(8,128)S(1)}, u32[]{:S(2)}, u32[]{:S(2)}) %collective-permute-start.7) | collective-permute-done | bytes 65568 | tf_op jit(solution)/shard_map/ppermute | solution.py:22
  27.2 0.0 collective-permute-start.9
  27.2 1.5 %collective-permute-done.6.received = f32[128,128]{1,0:T(8,128)S(1)} collective-permute-done((f32[128,128]{1,0:T(8,128)S(1)}, f32[128,128]{1,0:T(8,128)S(1)}, u32[]{:S(2)}, u32[]{:S(2)}) %collective-permute-start.6) | collective-permute-done | bytes 65568 | tf_op jit(solution)/shard_map/ppermute | solution.py:22
  28.7 0.0 collective-permute-start.8
  28.8 1.7 %shard_map.103.refs_4_ = f32[16,128,512]{2,1,0:T(8,128)} custom-call(f32[16,128,256]{2,1,0:T(8,128)S(1)} %get-tuple-element.31.solved, bf16[16,128,384]{2,1,0:T(8,128)(2,1)S(1)} %get-tuple-element.27.gains, f32[128,128]{1,0:T(8,128)S(1)} %collective-permute-done.9.theirs, f32[128,128]{1,0:T(8,128)S(1)} %shard_map.101.after.mine.refs_2_), custom_call_target="tpu_custom_call" | custom-call | flops 402653184 | bytes 4194304 | tf_op jit(solution)/shard_map/pallas_call | solution.py:272
  30.5 1.7 %shard_map.104 = (f32[16,128,512]{2,1,0:T(8,128)}, f32[128,128]{1,0:T(8,128)}) custom-call(f32[16,128,256]{2,1,0:T(8,128)S(1)} %get-tuple-element.26.solved, bf16[16,128,384]{2,1,0:T(8,128)(2,1)S(1)} %get-tuple-element.27.gains, f32[128,128]{1,0:T(8,128)S(1)} %collective-permute-done.8.theirs, ...), custom_call_target="tpu_custom_call", output_to_operand_aliasing={{0}: (8, {})} | custom-call | flops 402653184 | bytes 4194304 | tf_op jit(solution)/shard_map/pallas_call | solution.py:272
  (16 shorter events, 0.1 us)
Async XLA Ops:
  6.0 1.5 %collective-permute-start = (f32[128,256]{1,0:T(8,128)S(1)}, f32[128,256]{1,0:T(8,128)S(1)}, u32[]{:S(2)}, u32[]{:S(2)}) collective-permute-start(f32[128,256]{1,0:T(8,128)S(1)} %get-tuple-element.19), channel_id=1, source_target_pairs={{0,1},{1,0},{2,3},{3,2},{4,5},{5,4},{6,7},{7,6},{8,9},{9,8},{10,11... | collective-permute-start | bytes 393224 | tf_op jit(solution)/shard_map/ppermute | solution.py:22
  6.5 4.0 %collective-permute-start.3 = (f32[128,128]{1,0:T(8,128)S(1)}, f32[128,128]{1,0:T(8,128)S(1)}, u32[]{:S(2)}, u32[]{:S(2)}) collective-permute-start(f32[128,128]{1,0:T(8,128)S(1)} %get-tuple-element.30), channel_id=1, source_target_pairs={{0,1},{1,0},{2,3},{3,2},{4,5},{5,4},{6,7},{7,6},{8,9},{9,8},{10,11... | collective-permute-start | bytes 196616 | tf_op jit(solution)/shard_map/ppermute | solution.py:22
  7.5 7.2 %collective-permute-start.1 = (f32[128,256]{1,0:T(8,128)S(1)}, f32[128,256]{1,0:T(8,128)S(1)}, u32[]{:S(2)}, u32[]{:S(2)}) collective-permute-start(f32[128,256]{1,0:T(8,128)S(1)} %add.6.kept), channel_id=1, source_target_pairs={{0,2},{1,3},{2,0},{3,1},{4,6},{5,7},{6,4},{7,5},{8,10},{9,11},{10,... | collective-permute-start | bytes 393224 | tf_op jit(solution)/shard_map/ppermute | solution.py:22
  10.5 6.6 %collective-permute-start.4 = (f32[128,128]{1,0:T(8,128)S(1)}, f32[128,128]{1,0:T(8,128)S(1)}, u32[]{:S(2)}, u32[]{:S(2)}) collective-permute-start(f32[128,128]{1,0:T(8,128)S(1)} %add.7.kept), channel_id=1, source_target_pairs={{0,2},{1,3},{2,0},{3,1},{4,6},{5,7},{6,4},{7,5},{8,10},{9,11},{10,... | collective-permute-start | bytes 196616 | tf_op jit(solution)/shard_map/ppermute | solution.py:22
  10.6 4.2 %copy-start = (f32[1,128,512]{2,1,0:T(8,128)S(1)}, f32[1,128,512]{2,1,0:T(8,128)}, u32[]{:S(2)}) copy-start(f32[1,128,512]{2,1,0:T(8,128)} %param.13) | copy-start | bytes 786436
  10.6 4.2 %copy-start.1 = (f32[1,128,128]{2,1,0:T(8,128)S(1)}, f32[1,128,128]{2,1,0:T(8,128)}, u32[]{:S(2)}) copy-start(f32[1,128,128]{2,1,0:T(8,128)} %param.14) | copy-start | bytes 196612
  10.6 4.2 %copy-start.2 = (f32[1,128,128]{2,1,0:T(8,128)S(1)}, f32[1,128,128]{2,1,0:T(8,128)}, u32[]{:S(2)}) copy-start(f32[1,128,128]{2,1,0:T(8,128)} %param.15) | copy-start | bytes 196612
  15.0 5.4 %collective-permute-start.2 = (f32[128,256]{1,0:T(8,128)S(1)}, f32[128,256]{1,0:T(8,128)S(1)}, u32[]{:S(2)}, u32[]{:S(2)}) collective-permute-start(f32[128,256]{1,0:T(8,128)S(1)} %shard_map.97.after), channel_id=1, source_target_pairs={{0,4},{4,0},{8,12},{12,8},{1,5},{5,1},{9,13},{13,9},{2,6},{6,2},{1... | collective-permute-start | bytes 393224 | tf_op jit(solution)/shard_map/ppermute | solution.py:22
  17.3 6.1 %collective-permute-start.5 = (f32[128,128]{1,0:T(8,128)S(1)}, f32[128,128]{1,0:T(8,128)S(1)}, u32[]{:S(2)}, u32[]{:S(2)}) collective-permute-start(f32[128,128]{1,0:T(8,128)S(1)} %shard_map.98.after.mine.refs_3_), channel_id=1, source_target_pairs={{0,4},{4,0},{8,12},{12,8},{1,5},{5,1},{9,13},{13,9},{2,6},{6,2},{1... | collective-permute-start | bytes 196616 | tf_op jit(solution)/shard_map/ppermute | solution.py:22
  20.6 6.6 %collective-permute-start.7 = (f32[128,128]{1,0:T(8,128)S(1)}, f32[128,128]{1,0:T(8,128)S(1)}, u32[]{:S(2)}, u32[]{:S(2)}) collective-permute-start(f32[128,128]{1,0:T(8,128)S(1)} %shard_map.99.after), channel_id=1, source_target_pairs={{0,8},{4,12},{8,0},{12,4},{1,9},{5,13},{9,1},{13,5},{2,10},{6,14},... | collective-permute-start | bytes 196616 | tf_op jit(solution)/shard_map/ppermute | solution.py:22
  23.5 5.2 %collective-permute-start.6 = (f32[128,128]{1,0:T(8,128)S(1)}, f32[128,128]{1,0:T(8,128)S(1)}, u32[]{:S(2)}, u32[]{:S(2)}) collective-permute-start(f32[128,128]{1,0:T(8,128)S(1)} %shard_map.100.after), channel_id=1, source_target_pairs={{0,8},{4,12},{8,0},{12,4},{1,9},{5,13},{9,1},{13,5},{2,10},{6,14},... | collective-permute-start | bytes 196616 | tf_op jit(solution)/shard_map/ppermute | solution.py:22
  27.2 1.5 %collective-permute-start.9 = (f32[128,128]{1,0:T(8,128)S(1)}, f32[128,128]{1,0:T(8,128)S(1)}, u32[]{:S(2)}, u32[]{:S(2)}) collective-permute-start(f32[128,128]{1,0:T(8,128)S(1)} %shard_map.101.after.mine.refs_2_), channel_id=1, source_target_pairs={{0,1},{1,0},{2,3},{3,2},{4,5},{5,4},{6,7},{7,6},{8,9},{9,8},{10,11... | collective-permute-start | bytes 196616 | tf_op jit(solution)/shard_map/ppermute | solution.py:22
  28.7 1.7 %collective-permute-start.8 = (f32[128,128]{1,0:T(8,128)S(1)}, f32[128,128]{1,0:T(8,128)S(1)}, u32[]{:S(2)}, u32[]{:S(2)}) collective-permute-start(f32[128,128]{1,0:T(8,128)S(1)} %shard_map.102.mine), channel_id=1, source_target_pairs={{0,1},{1,0},{2,3},{3,2},{4,5},{5,4},{6,7},{7,6},{8,9},{9,8},{10,11... | collective-permute-start | bytes 196616 | tf_op jit(solution)/shard_map/ppermute | solution.py:22

commit v5 on v4

v5 whole, which is shorter than its diff:
```python
import functools

import jax
import jax.numpy as jnp
from jax import lax
from jax.experimental import pallas as pl
from jax.experimental.pallas import tpu as pltpu
from jax.sharding import PartitionSpec as P

F32 = jnp.float32
BF16 = jnp.bfloat16
LANES = 128
VMEM = pltpu.MemorySpace.VMEM
IN_VMEM = pl.BlockSpec(memory_space=pltpu.VMEM)
IN_HBM = pl.BlockSpec(memory_space=pl.ANY)
GROUP = 4
SMALL = 4 << 20


def swapped(block, axis, bit):
    route = [(i, i ^ bit) for i in range(lax.axis_size(axis))]
    return lax.ppermute(block, axis, route)


def parts_of(block):
    high = block.astype(BF16)
    return high, (block - high.astype(F32)).astype(BF16)


def matmul(left, right):
    return lax.dot_general(left, right, (((1,), (0,)), ((), ())), preferred_element_type=F32)


def left_of(block):
    high, low = parts_of(block)
    return jnp.concatenate([high, low, high], 1)


def right_of(block):
    high, low = parts_of(block)
    return jnp.concatenate([high, high, low], 0)


def product(left, right):
    return matmul(left_of(left), right_of(right))


def starts(tiles, which):
    if tiles == 4:
        return [which * LANES, which * LANES + 2 * LANES]
    return [which * 2 * LANES, which * 2 * LANES + LANES]


def lanes(start):
    return pl.ds(pl.multiple_of(start, LANES), LANES)


def fetched(rhs, starts_of, right, first, sems):
    rows = []
    for k in range(rhs.shape[0] // GROUP):
        some = pl.ds(k * GROUP, GROUP)
        row = []
        for j, start in enumerate(starts_of):
            row.append(pltpu.make_async_copy(rhs.at[some, :, lanes(start)], right.at[some, :, pl.ds((first + j) * LANES, LANES)], sems.at[k, first + j]))
        rows.append(row)
    return rows


def summed(lefts, right, highs, lows, copies):
    total = None
    for k, row in enumerate(copies):
        for copy in row:
            copy.wait()
        stacked = []
        for leaf in range(k * GROUP, k * GROUP + GROUP):
            high, low = parts_of(right[leaf])
            highs[leaf] = high
            lows[leaf] = low
            stacked += [high, high, low]
        here = matmul(lefts(k), jnp.concatenate(stacked, 0))
        total = here if total is None else total + here
    return total


def reduce_kernel(tiles, pattern, rhs, inverse, coupling, update, sent, kept, lefts, highs, lows, inverses, rest, right, tiles_a, tiles_b, flags, sems, sems_r, sems_b, flag_sem):
    leaves, rows = rhs.shape[:2]
    core = lax.rem(lax.axis_index("tile"), 2)
    flag_copy = pltpu.make_async_copy(pattern, flags, flag_sem)
    flag_copy.start()
    other, own = starts(tiles, 1 - core), starts(tiles, core)
    copies = []
    for k in range(leaves // GROUP):
        some = pl.ds(k * GROUP, GROUP)
        pair = [
            pltpu.make_async_copy(update.at[some], tiles_a.at[some], sems.at[k, 0]),
            pltpu.make_async_copy(inverse.at[some], tiles_b.at[some], sems.at[k, 1]),
        ]
        for copy in pair:
            copy.start()
        copies.append(pair)
    blocks = fetched(rhs, [other[0], own[0]], right, 1, sems_r)
    for k, row in enumerate(blocks):
        some = pl.ds(k * GROUP, GROUP)
        row.insert(0, pltpu.make_async_copy(coupling.at[some], right.at[some, :, pl.ds(0, LANES)], sems_r.at[k, 0]))
    later = fetched(rhs, [other[1], own[1]], rest, 0, sems_b)
    flag_copy.wait()
    for k in range(leaves // GROUP):
        for copy in copies[k]:
            copy.wait()
        for copy in blocks[k]:
            copy.start()
        for leaf in range(k * GROUP, k * GROUP + GROUP):
            inv_high, inv_low = parts_of(tiles_b[leaf])
            inverses[leaf] = jnp.concatenate([inv_high, inv_low, inv_high], 1)
            masked = tiles_a[leaf] * flags[0, leaf].astype(F32)
            here = matmul(left_of(masked), jnp.concatenate([inv_high, inv_high, inv_low], 0))
            lefts[:, pl.ds(leaf * 3 * rows, 3 * rows)] = left_of(here)
    total = None
    for k, row in enumerate(blocks):
        for copy in row:
            copy.wait()
        for copy in later[k]:
            copy.start()
        here = summed(lefts, right, highs, lows, k)
        total = here if total is None else total + here
    sent[...] = total[:, : 2 * LANES]
    kept[...] = jnp.concatenate([total[:, :LANES], total[:, 2 * LANES :]], 1)
    for row in later:
        for copy in row:
            copy.wait()


def summed(lefts, right, highs, lows, k):
    rows = lefts.shape[0]
    span = GROUP * 3 * rows
    stacked = []
    for leaf in range(k * GROUP, k * GROUP + GROUP):
        high, low = parts_of(right[leaf])
        highs[leaf] = high
        lows[leaf] = low
        stacked += [high, high, low]
    return matmul(lefts[:, pl.ds(k * span, span)], jnp.concatenate(stacked, 0))


def reduced(tiles, pattern, rhs, inverse, coupling, update):
    leaves, rows, columns = rhs.shape
    half = columns // 2
    wide = rows + half
    return pl.pallas_call(
        functools.partial(reduce_kernel, tiles),
        out_shape=(
            VMEM((rows, 2 * LANES), F32),
            VMEM((rows, 2 * LANES), F32),
            VMEM((rows, leaves * 3 * rows), BF16),
            VMEM((leaves, rows, wide), BF16),
            VMEM((leaves, rows, wide), BF16),
            VMEM((leaves, rows, 3 * rows), BF16),
            VMEM((leaves, rows, half), F32),
        ),
        in_specs=[IN_HBM] * 5,
        out_specs=(IN_VMEM,) * 7,
        scratch_shapes=[
            pltpu.VMEM((leaves, rows, wide), F32),
            pltpu.VMEM((leaves, rows, rows), F32),
            pltpu.VMEM((leaves, rows, rows), F32),
            pltpu.SMEM(pattern.shape, jnp.int32),
            pltpu.SemaphoreType.DMA((leaves // GROUP, 2)),
            pltpu.SemaphoreType.DMA((leaves // GROUP, 3)),
            pltpu.SemaphoreType.DMA((leaves // GROUP, 2)),
            pltpu.SemaphoreType.DMA,
        ],
        compiler_params=pltpu.CompilerParams(vmem_limit_bytes=48 << 20),
    )(pattern, rhs, inverse, coupling, update)


def second_kernel(lefts, rest, sent, kept, highs, lows):
    total = None
    for k in range(rest.shape[0] // GROUP):
        here = summed(lefts, rest, highs, lows, k)
        total = here if total is None else total + here
    sent[...] = total[:, :LANES]
    kept[...] = total[:, LANES:]


def second_reduced(lefts, rest):
    leaves, rows, half = rest.shape
    return pl.pallas_call(
        second_kernel,
        out_shape=(
            VMEM((rows, LANES), F32),
            VMEM((rows, LANES), F32),
            VMEM((leaves, rows, half), BF16),
            VMEM((leaves, rows, half), BF16),
        ),
        in_specs=[IN_VMEM] * 2,
        out_specs=(IN_VMEM,) * 4,
        compiler_params=pltpu.CompilerParams(vmem_limit_bytes=8 << 20),
        cost_estimate=pl.CostEstimate(flops=6 * leaves * rows * rows * half, bytes_accessed=leaves * rows * half * 8, transcendentals=0),
    )(lefts, rest)


def free_kernel(highs_a, lows_a, highs_b, lows_b, inverses, after, solved_a, solved_b, gains, token):
    for leaf in range(highs_a.shape[0]):
        left = inverses[leaf]
        high = highs_a[leaf]
        here = matmul(left, jnp.concatenate([high, high, lows_a[leaf]], 0))
        gains[leaf] = left_of(here[:, :LANES])
        solved_a[leaf] = here[:, LANES:]
        high = highs_b[leaf]
        solved_b[leaf] = matmul(left, jnp.concatenate([high, high, lows_b[leaf]], 0))
    token[...] = jnp.zeros_like(token)


def freed(highs_a, lows_a, highs_b, lows_b, inverses, after):
    leaves, rows, wide = highs_a.shape
    half = highs_b.shape[2]
    return pl.pallas_call(
        free_kernel,
        out_shape=(
            VMEM((leaves, rows, half), F32),
            VMEM((leaves, rows, half), F32),
            VMEM((leaves, rows, 3 * rows), BF16),
            VMEM((8, LANES), F32),
        ),
        in_specs=[IN_VMEM] * 6,
        out_specs=(IN_VMEM,) * 4,
        compiler_params=pltpu.CompilerParams(vmem_limit_bytes=8 << 20),
        cost_estimate=pl.CostEstimate(flops=6 * leaves * rows * rows * (wide + half), bytes_accessed=leaves * rows * wide * 12, transcendentals=0),
    )(highs_a, lows_a, highs_b, lows_b, inverses, after)


def small(kernel, out_shape, *operands):
    return pl.pallas_call(
        kernel,
        out_shape=out_shape,
        in_specs=[IN_VMEM] * len(operands),
        out_specs=jax.tree.map(lambda _: IN_VMEM, out_shape),
        compiler_params=pltpu.CompilerParams(vmem_limit_bytes=SMALL),
    )(*operands)


def map_kernel(tiles, received, kept, sep_rhs, sep_inverse, sep_coupling, mapped):
    start = starts(tiles, lax.rem(lax.axis_index("tile"), 2))[0]
    right = jnp.concatenate([sep_coupling[...], sep_rhs[:, lanes(start)]], 1)
    mapped[...] = product(sep_inverse[...], right - (received[...] + kept[...]))


def offset_kernel(tiles, received, kept, sep_rhs, sep_inverse, after, offset):
    start = starts(tiles, lax.rem(lax.axis_index("tile"), 2))[1]
    offset[...] = product(sep_inverse[...], sep_rhs[:, lanes(start)] - (received[...] + kept[...]))


def pair_kernel(mine_step, mine, other_step, other, after, whole):
    @pl.when(lax.rem(lax.axis_index("chain"), 2) == 1)
    def _():
        whole[...] = mine[...] - product(mine_step[...], other[...])

    @pl.when(lax.rem(lax.axis_index("chain"), 2) == 0)
    def _():
        whole[...] = other[...] - product(other_step[...], mine[...])


def carry_kernel(other_step, other, received, after, carry):
    section = lax.axis_index("chain")

    @pl.when(section == 0)
    def _():
        carry[...] = jnp.zeros_like(carry)

    @pl.when(section == 1)
    def _():
        carry[...] = other[...]

    @pl.when(section == 2)
    def _():
        carry[...] = received[...]

    @pl.when(section == 3)
    def _():
        carry[...] = other[...] - product(other_step[...], received[...])


def affine_kernel(step, block, offset, result):
    result[...] = offset[...] - product(step[...], block[...])


def affine(step, block, offset):
    return small(affine_kernel, VMEM(offset.shape, F32), step, block, offset)


def scanned(section, solved, half):
    sections = lax.axis_size("chain")
    whole_b, whole_a = solved[:, :half], solved[:, half:]
    before_b, before_a = jnp.zeros_like(whole_b), -jnp.eye(whole_a.shape[0], dtype=F32)
    nothing = jnp.zeros_like(whole_a)
    bit = 1
    while bit < sections:
        upper = (section // bit) % 2 == 1
        other = swapped(jnp.concatenate([whole_b, whole_a], 1), "chain", bit)
        other_b, other_a = other[:, :half], other[:, half:]
        before_b = jnp.where(upper, affine(before_a, other_b, before_b), before_b)
        before_a = jnp.where(upper, affine(before_a, other_a, nothing), before_a)
        first_b, first_a = jnp.where(upper, other_b, whole_b), jnp.where(upper, other_a, whole_a)
        second_b, second_a = jnp.where(upper, whole_b, other_b), jnp.where(upper, whole_a, other_a)
        whole_b = affine(second_a, first_b, second_b)
        whole_a = affine(second_a, first_a, nothing)
        bit *= 2
    return before_b


def last_kernel(tiles, blocks, shared, first, gains, *refs):
    leaves, rows = gains.shape[:2]
    count = len(blocks)
    core = lax.rem(lax.axis_index("tile"), 2)
    solved, carries, refs = refs[:count], refs[count : 2 * count], refs[2 * count :]
    copies = []
    if shared:
        step, offset_a, carry_a, offset_b, carry_b = refs[:5]
        out, share_out, values, sems, share, share_sem = refs[-6:]
        low = lax.axis_index("tile") < 2
        here = product(step[...], jnp.where(low, carry_a[...], carry_b[...]))
        share[...] = jnp.where(low, offset_a[...], offset_b[...]) - here
        copies.append(pltpu.make_async_copy(share, share_out, share_sem))
        copies[0].start()
    else:
        out, values, sems = refs[-4] if first else refs[-3], refs[-2], refs[-1]
    places = [starts(tiles, core if own else 1 - core)[chunk] for chunk, own in blocks]
    right = jnp.concatenate([right_of(carry[...]) for carry in carries], 1)
    for k in range(leaves // GROUP):
        for leaf in range(k * GROUP, k * GROUP + GROUP):
            here = matmul(gains[leaf], right)
            for j, (_, own) in enumerate(blocks):
                side = pl.ds(LANES if own else 0, LANES)
                values[j, leaf] = solved[j][leaf, :, side] - here[:, j * LANES : (j + 1) * LANES]
        some = pl.ds(k * GROUP, GROUP)
        for j, start in enumerate(places):
            copy = pltpu.make_async_copy(values.at[j, some], out.at[some, :, lanes(start)], sems.at[k, j])
            copy.start()
            copies.append(copy)
    if first:
        refs[-3][...] = jnp.zeros_like(refs[-3])
    for copy in copies:
        copy.wait()


def leaf_values(tiles, blocks, columns, gains, solved, carries, shared, *before):
    leaves, rows = gains.shape[:2]
    count = len(blocks)
    out_shape = [jax.ShapeDtypeStruct((leaves, rows, columns), F32)]
    out_specs = [IN_HBM]
    if not before:
        out_shape.append(VMEM((8, LANES), F32))
        out_specs.append(IN_VMEM)
    scratch = [pltpu.VMEM((count, leaves, rows, LANES), F32), pltpu.SemaphoreType.DMA((leaves // GROUP, count))]
    if shared:
        out_shape.append(jax.ShapeDtypeStruct((rows, LANES), F32))
        out_specs.append(IN_HBM)
        scratch += [pltpu.VMEM((rows, LANES), F32), pltpu.SemaphoreType.DMA]
    operands = 1 + 2 * count + len(shared)
    return pl.pallas_call(
        functools.partial(last_kernel, tiles, blocks, bool(shared), not before),
        out_shape=out_shape,
        in_specs=[IN_VMEM] * operands + [IN_HBM] * len(before),
        out_specs=out_specs,
        scratch_shapes=scratch,
        input_output_aliases={operands: 0} if before else {},
        compiler_params=pltpu.CompilerParams(vmem_limit_bytes=8 << 20),
        cost_estimate=pl.CostEstimate(flops=6 * leaves * rows * rows * LANES * count, bytes_accessed=leaves * rows * LANES * count * 8, transcendentals=0),
    )(gains, *solved, *carries, *shared, *before)


def shards(
    leaf_rhs,
    leaf_inverse,
    leaf_coupling,
    leaf_update,
    update_pattern,
    sep_rhs,
    sep_inverse,
    sep_coupling,
):
    tiles = lax.axis_size("tile")
    sections = lax.axis_size("chain")
    tile = lax.axis_index("tile")
    section = lax.axis_index("chain")
    columns = sep_rhs.shape[2]
    width = columns // tiles
    block = VMEM((sep_rhs.shape[1], LANES), F32)
    double = VMEM((sep_rhs.shape[1], 2 * LANES), F32)
    inverse, right = sep_inverse[0], sep_rhs[0]

    sent_a, kept_a, lefts, highs_a, lows_a, inverses, rest = reduced(
        tiles, update_pattern, leaf_rhs[0], leaf_inverse[0], leaf_coupling[0], leaf_update[0]
    )
    kept_a = kept_a + swapped(sent_a, "tile", 1)
    sent_b, kept_b, highs_b, lows_b = second_reduced(lefts, rest)
    kept_b = kept_b + swapped(sent_b, "tile", 1)
    received_a = swapped(kept_a, "tile", 2) if tiles > 2 else jnp.zeros_like(kept_a)
    received_b = swapped(kept_b, "tile", 2) if tiles > 2 else jnp.zeros_like(kept_b)
    bit = 4
    while bit < tiles:
        kept_a, kept_b = kept_a + received_a, kept_b + received_b
        received_a, received_b = swapped(kept_a, "tile", bit), swapped(kept_b, "tile", bit)
        bit *= 2
    mapped = small(functools.partial(map_kernel, tiles), double, received_a, kept_a, right, inverse, sep_coupling[0])
    offset_b = small(functools.partial(offset_kernel, tiles), block, received_b, kept_b, right, inverse, mapped)
    step, offset_a = mapped[:, :LANES], mapped[:, LANES:]
    if sections == 4:
        other = swapped(mapped, "chain", 1)
        other_step, other_a = other[:, :LANES], other[:, LANES:]
        other_b = swapped(offset_b, "chain", 1)
        whole_a = small(pair_kernel, block, step, offset_a, other_step, other_a, offset_b)
        met_a = swapped(whole_a, "chain", 2)
        whole_b = small(pair_kernel, block, step, offset_b, other_step, other_b, whole_a)
        met_b = swapped(whole_b, "chain", 2)
        solved_a, solved_b, gains, token = freed(highs_a, lows_a, highs_b, lows_b, inverses, whole_b)
        carry_a = small(carry_kernel, block, other_step, other_a, met_a, token)
        leaf_share, token = leaf_values(tiles, ((0, True),), columns, gains, [solved_a], [carry_a], ())
        carry_b = small(carry_kernel, block, other_step, other_b, met_b, token)
    else:
        solved_a, solved_b, gains, _ = freed(highs_a, lows_a, highs_b, lows_b, inverses, mapped)
        carry = scanned(section, jnp.concatenate([offset_a, offset_b, step], 1), 2 * LANES)
        carry_a, carry_b = carry[:, :LANES], carry[:, LANES:]
        leaf_share, _ = leaf_values(tiles, ((0, True),), columns, gains, [solved_a], [carry_a], ())
    theirs_a = swapped(carry_a, "tile", 1)
    theirs_b = swapped(carry_b, "tile", 1)
    shared = (step, offset_a, carry_a, offset_b, carry_b) if tiles == 4 else ()
    middle = leaf_values(tiles, ((0, False), (1, True)), columns, gains, [solved_a, solved_b], [theirs_a, carry_b], shared, leaf_share)
    (leaf_share,) = leaf_values(tiles, ((1, False),), columns, gains, [solved_b], [theirs_b], (), middle[0])
    if tiles == 4:
        sep_share = middle[1]
    else:
        own = affine(step, jnp.concatenate([carry_a, carry_b], 1), jnp.concatenate([offset_a, offset_b], 1))
        others = swapped(own, "tile", 1)
        lower = jnp.where(tile % 2 == 0, own, others)
        upper = jnp.where(tile % 2 == 0, others, own)
        sep_share = lax.dynamic_slice_in_dim(jnp.concatenate([lower, upper], 1), tile * width, width, 1)
    return (leaf_share[None], sep_share[None])


def solution(mesh):
    return jax.shard_map(
        shards,
        mesh=mesh,
        in_specs=(
            P(("parts", "chain"), "tile", None, None),
            P(("parts", "chain"), "tile", None, None),
            P(("parts", "chain"), "tile", None, None),
            P(("parts", "chain"), "tile", None, None),
            P(("parts", "chain"), "tile"),
            P(("parts", "chain"), None, None),
            P(("parts", "chain"), None, None),
            P(("parts", "chain"), None, None),
        ),
        out_specs=(P(("parts", "chain"), "tile", None, None), P(("parts", "chain"), None, "tile")),
        check_vma=False,
    )
```

time: 32.4 us -> 31.8 us (0.981)
  waiting for transfers between devices: 9.67 us -> 6.62 us
  starting transfers between devices: 10.4 us -> 11.7 us
  Pallas kernels: 11.4 us -> 12.5 us
    ppermute x10, waiting for transfers between devices: 9.67 us -> 6.62 us  [swapped(): return lax.ppermute(block, axis, route)]
    pallas_call x3 -> x5, Pallas kernels: 5.23 us -> 6.91 us  [the longest x3 4.34 us: leaf_values(): pl.pallas_call(functools.partial(last_kernel, tiles, blocks, bool(shared)...]
    ppermute x10, starting transfers between devices: 10.4 us -> 11.7 us  [swapped(): return lax.ppermute(block, axis, route)]
    pallas_call x1, Pallas kernels: 5.37 us -> 4.83 us  [reduced(): pl.pallas_call(functools.partial(reduce_kernel, tiles), out_shape=(VMEM((...]
  transfers between devices with their start and end apart: 10 -> 10, of which waited for: 5 -> 7; matrix products, arithmetic and copies ran while one was open for 0% -> 0% of each run, Pallas kernels for 13% -> 20%
where the time goes in v5:
time: 31.8 us; the launch traced here: 31.6 us
  Pallas kernels  12.5 us (39%)
  starting transfers between devices  11.7 us (37%)
  waiting for transfers between devices  6.62 us (21%)
  between operations  0.75 us (2%)
    ppermute x10, starting transfers between devices, swapped(): return lax.ppermute(block, axis, route)  11.7 us
    ppermute x10, waiting for transfers between devices, swapped(): return lax.ppermute(block, axis, route)  6.62 us
    pallas_call x1, Pallas kernels, reduced(): pl.pallas_call(functools.partial(reduce_kernel, tiles), out_shape=(VMEM((...  4.83 us
    pallas_call x3, Pallas kernels, leaf_values(): pl.pallas_call(functools.partial(last_kernel, tiles, blocks, bool(shared)...  4.34 us
    pallas_call x1, Pallas kernels, freed(): pl.pallas_call(free_kernel, out_shape=(VMEM((leaves, rows, half), F32), V...  1.82 us
    pallas_call x1, Pallas kernels, second_reduced(): pl.pallas_call(second_kernel, out_shape=(VMEM((rows, LANES), F32), VMEM((...  0.75 us
    pallas_call x6, Pallas kernels, small(): pl.pallas_call(kernel, out_shape=out_shape, in_specs=[IN_VMEM] * len(oper...  0.75 us
  transfers between devices with their start and end apart: 10, of which 7 were waited for; matrix products, arithmetic and copies ran while one was open for 0% of the time, Pallas kernels for 20%

profile of v5, /device:TPU:0, one launch (start us, length us, event | category | flops | bytes accessed | tf_op | source)
XLA Modules:
  0.0 31.6 jit_solution(6023689783538450654)
XLA Ops:
  0.6 4.8 %shard_map.95 = (f32[128,256]{1,0:T(8,128)S(1)}, f32[128,256]{1,0:T(8,128)S(1)}, bf16[128,6144]{1,0:T(8,128)(2,1)S(1)}, bf16[16,128,384]{2,1,0:T(8,128)(2,1)S(1)...) custom-call(s32[1,16]{1,0:T(1,128)} %pattern.1, ...), custom_call_target="tpu_custom_call" | custom-call | tf_op jit(solution)/shard_map/pallas_call | solution.py:149
  5.5 0.5 %collective-permute-start = (f32[128,256]{1,0:T(8,128)S(1)}, f32[128,256]{1,0:T(8,128)S(1)}, u32[]{:S(2)}, u32[]{:S(2)}) collective-permute-start(f32[128,256]{1,0:T(8,128)S(1)} %get-tuple-element.29), channel_id=1, source_target_pairs={{0,1},{1,0},{2,3},{3,2},{4,5},{5,4},{6,7},{7,6},{8,9},{9,8},{10,11... | collective-permute-start | bytes 393224 | tf_op jit(solution)/shard_map/ppermute | solution.py:22
  6.0 1.0 %collective-permute-done = f32[128,256]{1,0:T(8,128)S(1)} collective-permute-done((f32[128,256]{1,0:T(8,128)S(1)}, f32[128,256]{1,0:T(8,128)S(1)}, u32[]{:S(2)}, u32[]{:S(2)}) %collective-permute-start) | collective-permute-done | bytes 131104 | tf_op jit(solution)/shard_map/ppermute | solution.py:22
  7.0 2.9 %collective-permute-start.1 = (f32[128,256]{1,0:T(8,128)S(1)}, f32[128,256]{1,0:T(8,128)S(1)}, u32[]{:S(2)}, u32[]{:S(2)}) collective-permute-start(f32[128,256]{1,0:T(8,128)S(1)} %add.6.kept), channel_id=1, source_target_pairs={{0,2},{1,3},{2,0},{3,1},{4,6},{5,7},{6,4},{7,5},{8,10},{9,11},{10,... | collective-permute-start | bytes 393224 | tf_op jit(solution)/shard_map/ppermute | solution.py:22
  9.9 0.8 %shard_map.96 = (f32[128,128]{1,0:T(8,128)S(1)}, f32[128,128]{1,0:T(8,128)S(1)}, bf16[16,128,256]{2,1,0:T(8,128)(2,1)S(1)}, bf16[16,128,256]{2,1,0:T(8,128)(2,1)S(1)}) custom-call(bf16[128,6144]{1,0:T(8,128)(2,1)S(1)} %get-tuple-element.23.lefts, f32[16,128,256]{2,1,0:T(8,128)S(1)} %get-tuple-element.24.rest), custom_call_target="tpu_custom_call" | custom-call | flops 402653184 | bytes 4194304 | tf_op jit(solution)/shard_map/pallas_call | solution.py:187
  10.8 1.2 %collective-permute-done.2 = f32[128,128]{1,0:T(8,128)S(1)} collective-permute-done((f32[128,128]{1,0:T(8,128)S(1)}, f32[128,128]{1,0:T(8,128)S(1)}, u32[]{:S(2)}, u32[]{:S(2)}) %collective-permute-start.2) | collective-permute-done | bytes 65568 | tf_op jit(solution)/shard_map/ppermute | solution.py:22
  12.1 1.6 %collective-permute-done.1.received = f32[128,256]{1,0:T(8,128)S(1)} collective-permute-done((f32[128,256]{1,0:T(8,128)S(1)}, f32[128,256]{1,0:T(8,128)S(1)}, u32[]{:S(2)}, u32[]{:S(2)}) %collective-permute-start.1) | collective-permute-done | bytes 131104 | tf_op jit(solution)/shard_map/ppermute | solution.py:22
  13.8 0.2 shard_map.97.after
  14.0 1.9 %collective-permute-start.4 = (f32[128,256]{1,0:T(8,128)S(1)}, f32[128,256]{1,0:T(8,128)S(1)}, u32[]{:S(2)}, u32[]{:S(2)}) collective-permute-start(f32[128,256]{1,0:T(8,128)S(1)} %shard_map.97.after), channel_id=1, source_target_pairs={{0,4},{4,0},{8,12},{12,8},{1,5},{5,1},{9,13},{13,9},{2,6},{6,2},{1... | collective-permute-start | bytes 393224 | tf_op jit(solution)/shard_map/ppermute | solution.py:22
  15.8 0.5 %collective-permute-done.3.received = f32[128,128]{1,0:T(8,128)S(1)} collective-permute-done((f32[128,128]{1,0:T(8,128)S(1)}, f32[128,128]{1,0:T(8,128)S(1)}, u32[]{:S(2)}, u32[]{:S(2)}) %collective-permute-start.3) | collective-permute-done | bytes 65568 | tf_op jit(solution)/shard_map/ppermute | solution.py:22
  16.4 0.2 shard_map.98.after.mine.refs_7_
  16.6 1.6 %collective-permute-start.5 = (f32[128,128]{1,0:T(8,128)S(1)}, f32[128,128]{1,0:T(8,128)S(1)}, u32[]{:S(2)}, u32[]{:S(2)}) collective-permute-start(f32[128,128]{1,0:T(8,128)S(1)} %shard_map.98.after.mine.refs_7_), channel_id=1, source_target_pairs={{0,4},{4,0},{8,12},{12,8},{1,5},{5,1},{9,13},{13,9},{2,6},{6,2},{1... | collective-permute-start | bytes 196616 | tf_op jit(solution)/shard_map/ppermute | solution.py:22
  18.2 1.6 %collective-permute-done.4 = f32[128,256]{1,0:T(8,128)S(1)} collective-permute-done((f32[128,256]{1,0:T(8,128)S(1)}, f32[128,256]{1,0:T(8,128)S(1)}, u32[]{:S(2)}, u32[]{:S(2)}) %collective-permute-start.4) | collective-permute-done | bytes 131104 | tf_op jit(solution)/shard_map/ppermute | solution.py:22
  19.8 0.2 shard_map.99.after
  20.0 2.8 %collective-permute-start.7 = (f32[128,128]{1,0:T(8,128)S(1)}, f32[128,128]{1,0:T(8,128)S(1)}, u32[]{:S(2)}, u32[]{:S(2)}) collective-permute-start(f32[128,128]{1,0:T(8,128)S(1)} %shard_map.99.after), channel_id=1, source_target_pairs={{0,8},{4,12},{8,0},{12,4},{1,9},{5,13},{9,1},{13,5},{2,10},{6,14},... | collective-permute-start | bytes 196616 | tf_op jit(solution)/shard_map/ppermute | solution.py:22
  22.8 0.2 shard_map.100.after
  23.0 1.4 %collective-permute-start.6 = (f32[128,128]{1,0:T(8,128)S(1)}, f32[128,128]{1,0:T(8,128)S(1)}, u32[]{:S(2)}, u32[]{:S(2)}) collective-permute-start(f32[128,128]{1,0:T(8,128)S(1)} %shard_map.100.after), channel_id=1, source_target_pairs={{0,8},{4,12},{8,0},{12,4},{1,9},{5,13},{9,1},{13,5},{2,10},{6,14},... | collective-permute-start | bytes 196616 | tf_op jit(solution)/shard_map/ppermute | solution.py:22
  24.4 1.8 %shard_map.101 = (f32[16,128,256]{2,1,0:T(8,128)S(1)}, f32[16,128,256]{2,1,0:T(8,128)S(1)}, bf16[16,128,384]{2,1,0:T(8,128)(2,1)S(1)}, f32[8,128]{1,0:T(8,128)S(1)}) custom-call(bf16[16,128,384]{2,1,0:T(8,128)(2,1)S(1)} %get-tuple-element.21.highs_a, bf16[16,128,384]{2,1,0:T(8,128)(2,1)S(1)} %get-tuple-element.22.lows_a, ...), custom_call_target="tpu_custom_call" | custom-call | flops 1006632960 | bytes 9437184 | tf_op jit(solution)/shard_map/pallas_call | solution.py:217
  26.2 0.4 %collective-permute-done.7.received = f32[128,128]{1,0:T(8,128)S(1)} collective-permute-done((f32[128,128]{1,0:T(8,128)S(1)}, f32[128,128]{1,0:T(8,128)S(1)}, u32[]{:S(2)}, u32[]{:S(2)}) %collective-permute-start.7) | collective-permute-done | bytes 65568 | tf_op jit(solution)/shard_map/ppermute | solution.py:22
  26.6 1.3 %shard_map.103 = (f32[16,128,512]{2,1,0:T(8,128)}, f32[8,128]{1,0:T(8,128)S(1)}) custom-call(bf16[16,128,384]{2,1,0:T(8,128)(2,1)S(1)} %get-tuple-element.32.gains, f32[16,128,256]{2,1,0:T(8,128)S(1)} %get-tuple-element.34.refs_0_, f32[128,128]{1,0:T(8,128)S(1)} %shard_map.102.refs_1_.refs_6_), custom_call_target="tpu_custom_call" | custom-call | flops 201326592 | bytes 2097152 | tf_op jit(solution)/shard_map/pallas_call | solution.py:360
  28.0 0.2 collective-permute-done.6.received
  28.2 0.4 %collective-permute-start.8 = (f32[128,128]{1,0:T(8,128)S(1)}, f32[128,128]{1,0:T(8,128)S(1)}, u32[]{:S(2)}, u32[]{:S(2)}) collective-permute-start(f32[128,128]{1,0:T(8,128)S(1)} %shard_map.104.refs_3_.refs_8_), channel_id=1, source_target_pairs={{0,1},{1,0},{2,3},{3,2},{4,5},{5,4},{6,7},{7,6},{8,9},{9,8},{10,11... | collective-permute-start | bytes 196616 | tf_op jit(solution)/shard_map/ppermute | solution.py:22
  28.6 1.7 %shard_map.105 = (f32[16,128,512]{2,1,0:T(8,128)}, f32[128,128]{1,0:T(8,128)}) custom-call(bf16[16,128,384]{2,1,0:T(8,128)(2,1)S(1)} %get-tuple-element.32.gains, f32[16,128,256]{2,1,0:T(8,128)S(1)} %get-tuple-element.34.refs_0_, f32[16,128,256]{2,1,0:T(8,128)S(1)} %get-tuple-element.33.refs_1_.refs_0_, ...), custom_call_target="tpu_custom_call", output_to_operand_aliasing={{0}: (10, {})} | custom-call | flops 402653184 | bytes 4194304 | tf_op jit(solution)/shard_map/pallas_call | solution.py:360
  30.3 1.3 %shard_map.106 = f32[16,128,512]{2,1,0:T(8,128)} custom-call(bf16[16,128,384]{2,1,0:T(8,128)(2,1)S(1)} %get-tuple-element.32.gains, f32[16,128,256]{2,1,0:T(8,128)S(1)} %get-tuple-element.33.refs_1_.refs_0_, f32[128,128]{1,0:T(8,128)S(1)} %collective-permute-done.8.refs_1_, f32[16,128,512]{2,1,0:T(8,128)} %get-tuple-element.38.refs_2_), custom_call_target="tpu_custom_call", output_to_operand_aliasing={{}: (3, {})} | custom-call | flops 201326592 | bytes 2097152 | tf_op jit(solution)/shard_map/pallas_call | solution.py:360
  (18 shorter events, 0.2 us)
Async XLA Ops:
  5.5 1.5 %collective-permute-start = (f32[128,256]{1,0:T(8,128)S(1)}, f32[128,256]{1,0:T(8,128)S(1)}, u32[]{:S(2)}, u32[]{:S(2)}) collective-permute-start(f32[128,256]{1,0:T(8,128)S(1)} %get-tuple-element.29), channel_id=1, source_target_pairs={{0,1},{1,0},{2,3},{3,2},{4,5},{5,4},{6,7},{7,6},{8,9},{9,8},{10,11... | collective-permute-start | bytes 393224 | tf_op jit(solution)/shard_map/ppermute | solution.py:22
  7.0 6.8 %copy-start = (f32[1,128,512]{2,1,0:T(8,128)S(1)}, f32[1,128,512]{2,1,0:T(8,128)}, u32[]{:S(2)}) copy-start(f32[1,128,512]{2,1,0:T(8,128)} %param.13) | copy-start | bytes 786436
  7.0 6.8 %copy-start.1 = (f32[1,128,128]{2,1,0:T(8,128)S(1)}, f32[1,128,128]{2,1,0:T(8,128)}, u32[]{:S(2)}) copy-start(f32[1,128,128]{2,1,0:T(8,128)} %param.14) | copy-start | bytes 196612
  7.0 6.8 %copy-start.2 = (f32[1,128,128]{2,1,0:T(8,128)S(1)}, f32[1,128,128]{2,1,0:T(8,128)}, u32[]{:S(2)}) copy-start(f32[1,128,128]{2,1,0:T(8,128)} %param.15) | copy-start | bytes 196612
  7.0 6.8 %collective-permute-start.1 = (f32[128,256]{1,0:T(8,128)S(1)}, f32[128,256]{1,0:T(8,128)S(1)}, u32[]{:S(2)}, u32[]{:S(2)}) collective-permute-start(f32[128,256]{1,0:T(8,128)S(1)} %add.6.kept), channel_id=1, source_target_pairs={{0,2},{1,3},{2,0},{3,1},{4,6},{5,7},{6,4},{7,5},{8,10},{9,11},{10,... | collective-permute-start | bytes 393224 | tf_op jit(solution)/shard_map/ppermute | solution.py:22
  10.7 1.3 %collective-permute-start.2 = (f32[128,128]{1,0:T(8,128)S(1)}, f32[128,128]{1,0:T(8,128)S(1)}, u32[]{:S(2)}, u32[]{:S(2)}) collective-permute-start(f32[128,128]{1,0:T(8,128)S(1)} %get-tuple-element.31), channel_id=1, source_target_pairs={{0,1},{1,0},{2,3},{3,2},{4,5},{5,4},{6,7},{7,6},{8,9},{9,8},{10,11... | collective-permute-start | bytes 196616 | tf_op jit(solution)/shard_map/ppermute | solution.py:22
  12.0 4.3 %collective-permute-start.3 = (f32[128,128]{1,0:T(8,128)S(1)}, f32[128,128]{1,0:T(8,128)S(1)}, u32[]{:S(2)}, u32[]{:S(2)}) collective-permute-start(f32[128,128]{1,0:T(8,128)S(1)} %add.7.kept), channel_id=1, source_target_pairs={{0,2},{1,3},{2,0},{3,1},{4,6},{5,7},{6,4},{7,5},{8,10},{9,11},{10,... | collective-permute-start | bytes 196616 | tf_op jit(solution)/shard_map/ppermute | solution.py:22
  14.0 5.8 %collective-permute-start.4 = (f32[128,256]{1,0:T(8,128)S(1)}, f32[128,256]{1,0:T(8,128)S(1)}, u32[]{:S(2)}, u32[]{:S(2)}) collective-permute-start(f32[128,256]{1,0:T(8,128)S(1)} %shard_map.97.after), channel_id=1, source_target_pairs={{0,4},{4,0},{8,12},{12,8},{1,5},{5,1},{9,13},{13,9},{2,6},{6,2},{1... | collective-permute-start | bytes 393224 | tf_op jit(solution)/shard_map/ppermute | solution.py:22
  16.6 6.2 %collective-permute-start.5 = (f32[128,128]{1,0:T(8,128)S(1)}, f32[128,128]{1,0:T(8,128)S(1)}, u32[]{:S(2)}, u32[]{:S(2)}) collective-permute-start(f32[128,128]{1,0:T(8,128)S(1)} %shard_map.98.after.mine.refs_7_), channel_id=1, source_target_pairs={{0,4},{4,0},{8,12},{12,8},{1,5},{5,1},{9,13},{13,9},{2,6},{6,2},{1... | collective-permute-start | bytes 196616 | tf_op jit(solution)/shard_map/ppermute | solution.py:22
  20.0 6.6 %collective-permute-start.7 = (f32[128,128]{1,0:T(8,128)S(1)}, f32[128,128]{1,0:T(8,128)S(1)}, u32[]{:S(2)}, u32[]{:S(2)}) collective-permute-start(f32[128,128]{1,0:T(8,128)S(1)} %shard_map.99.after), channel_id=1, source_target_pairs={{0,8},{4,12},{8,0},{12,4},{1,9},{5,13},{9,1},{13,5},{2,10},{6,14},... | collective-permute-start | bytes 196616 | tf_op jit(solution)/shard_map/ppermute | solution.py:22
  23.0 5.2 %collective-permute-start.6 = (f32[128,128]{1,0:T(8,128)S(1)}, f32[128,128]{1,0:T(8,128)S(1)}, u32[]{:S(2)}, u32[]{:S(2)}) collective-permute-start(f32[128,128]{1,0:T(8,128)S(1)} %shard_map.100.after), channel_id=1, source_target_pairs={{0,8},{4,12},{8,0},{12,4},{1,9},{5,13},{9,1},{13,5},{2,10},{6,14},... | collective-permute-start | bytes 196616 | tf_op jit(solution)/shard_map/ppermute | solution.py:22
  26.6 1.9 %collective-permute-start.9 = (f32[128,128]{1,0:T(8,128)S(1)}, f32[128,128]{1,0:T(8,128)S(1)}, u32[]{:S(2)}, u32[]{:S(2)}) collective-permute-start(f32[128,128]{1,0:T(8,128)S(1)} %shard_map.102.refs_1_.refs_6_), channel_id=1, source_target_pairs={{0,1},{1,0},{2,3},{3,2},{4,5},{5,4},{6,7},{7,6},{8,9},{9,8},{10,11... | collective-permute-start | bytes 196616 | tf_op jit(solution)/shard_map/ppermute | solution.py:22
  28.2 2.1 %collective-permute-start.8 = (f32[128,128]{1,0:T(8,128)S(1)}, f32[128,128]{1,0:T(8,128)S(1)}, u32[]{:S(2)}, u32[]{:S(2)}) collective-permute-start(f32[128,128]{1,0:T(8,128)S(1)} %shard_map.104.refs_3_.refs_8_), channel_id=1, source_target_pairs={{0,1},{1,0},{2,3},{3,2},{4,5},{5,4},{6,7},{7,6},{8,9},{9,8},{10,11... | collective-permute-start | bytes 196616 | tf_op jit(solution)/shard_map/ppermute | solution.py:22

commit v6 on v5

--- a/solution.py
+++ b/solution.py
@@ -102,12 +102,15 @@
     for k, row in enumerate(blocks):
         some = pl.ds(k * GROUP, GROUP)
         row.insert(0, pltpu.make_async_copy(coupling.at[some], right.at[some, :, pl.ds(0, LANES)], sems_r.at[k, 0]))
+    for row in blocks[:2]:
+        for copy in row:
+            copy.start()
     later = fetched(rhs, [other[1], own[1]], rest, 0, sems_b)
     flag_copy.wait()
     for k in range(leaves // GROUP):
         for copy in copies[k]:
             copy.wait()
-        for copy in blocks[k]:
+        for copy in blocks[k + 2] if k + 2 < len(blocks) else later[k + 2 - len(blocks)]:
             copy.start()
         for leaf in range(k * GROUP, k * GROUP + GROUP):
             inv_high, inv_low = parts_of(tiles_b[leaf])
@@ -119,8 +122,9 @@
     for k, row in enumerate(blocks):
         for copy in row:
             copy.wait()
-        for copy in later[k]:
-            copy.start()
+        if k + 2 < len(later):
+            for copy in later[k + 2]:
+                copy.start()
         here = summed(lefts, right, highs, lows, k)
         total = here if total is None else total + here
     sent[...] = total[:, : 2 * LANES]

time: 31.8 us -> 30.9 us (0.972)
  Pallas kernels: 12.5 us -> 11.6 us
    pallas_call x1, Pallas kernels: 4.83 us -> 3.94 us  [reduced(): pl.pallas_call(functools.partial(reduce_kernel, tiles), out_shape=(VMEM((...]
  transfers between devices with their start and end apart: 10 -> 10, of which waited for: 7 -> 7; matrix products, arithmetic and copies ran while one was open for 0% -> 0% of each run, Pallas kernels for 20% -> 21%
where the time goes in v6:
time: 30.9 us; the launch traced here: 30.7 us
  starting transfers between devices  11.7 us (38%)
  Pallas kernels  11.6 us (38%)
  waiting for transfers between devices  6.62 us (21%)
  between operations  0.75 us (2%)
    ppermute x10, starting transfers between devices, swapped(): return lax.ppermute(block, axis, route)  11.7 us
    ppermute x10, waiting for transfers between devices, swapped(): return lax.ppermute(block, axis, route)  6.62 us
    pallas_call x3, Pallas kernels, leaf_values(): pl.pallas_call(functools.partial(last_kernel, tiles, blocks, bool(shared)...  4.34 us
    pallas_call x1, Pallas kernels, reduced(): pl.pallas_call(functools.partial(reduce_kernel, tiles), out_shape=(VMEM((...  3.94 us
    pallas_call x1, Pallas kernels, freed(): pl.pallas_call(free_kernel, out_shape=(VMEM((leaves, rows, half), F32), V...  1.82 us
    pallas_call x1, Pallas kernels, second_reduced(): pl.pallas_call(second_kernel, out_shape=(VMEM((rows, LANES), F32), VMEM((...  0.75 us
    pallas_call x6, Pallas kernels, small(): pl.pallas_call(kernel, out_shape=out_shape, in_specs=[IN_VMEM] * len(oper...  0.75 us
  transfers between devices with their start and end apart: 10, of which 7 were waited for; matrix products, arithmetic and copies ran while one was open for 0% of the time, Pallas kernels for 21%

profile of v6, /device:TPU:0, one launch (start us, length us, event | category | flops | bytes accessed | tf_op | source)
XLA Modules:
  0.0 30.7 jit_solution(1564123038973750091)
XLA Ops:
  0.6 3.9 %shard_map.95 = (f32[128,256]{1,0:T(8,128)S(1)}, f32[128,256]{1,0:T(8,128)S(1)}, bf16[128,6144]{1,0:T(8,128)(2,1)S(1)}, bf16[16,128,384]{2,1,0:T(8,128)(2,1)S(1)...) custom-call(s32[1,16]{1,0:T(1,128)} %pattern.1, ...), custom_call_target="tpu_custom_call" | custom-call | tf_op jit(solution)/shard_map/pallas_call | solution.py:153
  4.6 0.5 %collective-permute-start = (f32[128,256]{1,0:T(8,128)S(1)}, f32[128,256]{1,0:T(8,128)S(1)}, u32[]{:S(2)}, u32[]{:S(2)}) collective-permute-start(f32[128,256]{1,0:T(8,128)S(1)} %get-tuple-element.29), channel_id=1, source_target_pairs={{0,1},{1,0},{2,3},{3,2},{4,5},{5,4},{6,7},{7,6},{8,9},{9,8},{10,11... | collective-permute-start | bytes 393224 | tf_op jit(solution)/shard_map/ppermute | solution.py:22
  5.1 1.0 %collective-permute-done = f32[128,256]{1,0:T(8,128)S(1)} collective-permute-done((f32[128,256]{1,0:T(8,128)S(1)}, f32[128,256]{1,0:T(8,128)S(1)}, u32[]{:S(2)}, u32[]{:S(2)}) %collective-permute-start) | collective-permute-done | bytes 131104 | tf_op jit(solution)/shard_map/ppermute | solution.py:22
  6.1 2.9 %collective-permute-start.1 = (f32[128,256]{1,0:T(8,128)S(1)}, f32[128,256]{1,0:T(8,128)S(1)}, u32[]{:S(2)}, u32[]{:S(2)}) collective-permute-start(f32[128,256]{1,0:T(8,128)S(1)} %add.6.kept), channel_id=1, source_target_pairs={{0,2},{1,3},{2,0},{3,1},{4,6},{5,7},{6,4},{7,5},{8,10},{9,11},{10,... | collective-permute-start | bytes 393224 | tf_op jit(solution)/shard_map/ppermute | solution.py:22
  9.1 0.8 %shard_map.96 = (f32[128,128]{1,0:T(8,128)S(1)}, f32[128,128]{1,0:T(8,128)S(1)}, bf16[16,128,256]{2,1,0:T(8,128)(2,1)S(1)}, bf16[16,128,256]{2,1,0:T(8,128)(2,1)S(1)}) custom-call(bf16[128,6144]{1,0:T(8,128)(2,1)S(1)} %get-tuple-element.23.lefts, f32[16,128,256]{2,1,0:T(8,128)S(1)} %get-tuple-element.24.rest), custom_call_target="tpu_custom_call" | custom-call | flops 402653184 | bytes 4194304 | tf_op jit(solution)/shard_map/pallas_call | solution.py:191
  9.9 1.2 %collective-permute-done.2 = f32[128,128]{1,0:T(8,128)S(1)} collective-permute-done((f32[128,128]{1,0:T(8,128)S(1)}, f32[128,128]{1,0:T(8,128)S(1)}, u32[]{:S(2)}, u32[]{:S(2)}) %collective-permute-start.2) | collective-permute-done | bytes 65568 | tf_op jit(solution)/shard_map/ppermute | solution.py:22
  11.2 1.6 %collective-permute-done.1.received = f32[128,256]{1,0:T(8,128)S(1)} collective-permute-done((f32[128,256]{1,0:T(8,128)S(1)}, f32[128,256]{1,0:T(8,128)S(1)}, u32[]{:S(2)}, u32[]{:S(2)}) %collective-permute-start.1) | collective-permute-done | bytes 131104 | tf_op jit(solution)/shard_map/ppermute | solution.py:22
  12.9 0.2 shard_map.97.after
  13.1 1.9 %collective-permute-start.4 = (f32[128,256]{1,0:T(8,128)S(1)}, f32[128,256]{1,0:T(8,128)S(1)}, u32[]{:S(2)}, u32[]{:S(2)}) collective-permute-start(f32[128,256]{1,0:T(8,128)S(1)} %shard_map.97.after), channel_id=1, source_target_pairs={{0,4},{4,0},{8,12},{12,8},{1,5},{5,1},{9,13},{13,9},{2,6},{6,2},{1... | collective-permute-start | bytes 393224 | tf_op jit(solution)/shard_map/ppermute | solution.py:22
  14.9 0.5 %collective-permute-done.3.received = f32[128,128]{1,0:T(8,128)S(1)} collective-permute-done((f32[128,128]{1,0:T(8,128)S(1)}, f32[128,128]{1,0:T(8,128)S(1)}, u32[]{:S(2)}, u32[]{:S(2)}) %collective-permute-start.3) | collective-permute-done | bytes 65568 | tf_op jit(solution)/shard_map/ppermute | solution.py:22
  15.5 0.2 shard_map.98.after.mine.refs_7_
  15.7 1.6 %collective-permute-start.5 = (f32[128,128]{1,0:T(8,128)S(1)}, f32[128,128]{1,0:T(8,128)S(1)}, u32[]{:S(2)}, u32[]{:S(2)}) collective-permute-start(f32[128,128]{1,0:T(8,128)S(1)} %shard_map.98.after.mine.refs_7_), channel_id=1, source_target_pairs={{0,4},{4,0},{8,12},{12,8},{1,5},{5,1},{9,13},{13,9},{2,6},{6,2},{1... | collective-permute-start | bytes 196616 | tf_op jit(solution)/shard_map/ppermute | solution.py:22
  17.3 1.6 %collective-permute-done.4 = f32[128,256]{1,0:T(8,128)S(1)} collective-permute-done((f32[128,256]{1,0:T(8,128)S(1)}, f32[128,256]{1,0:T(8,128)S(1)}, u32[]{:S(2)}, u32[]{:S(2)}) %collective-permute-start.4) | collective-permute-done | bytes 131104 | tf_op jit(solution)/shard_map/ppermute | solution.py:22
  18.9 0.2 shard_map.99.after
  19.1 2.8 %collective-permute-start.7 = (f32[128,128]{1,0:T(8,128)S(1)}, f32[128,128]{1,0:T(8,128)S(1)}, u32[]{:S(2)}, u32[]{:S(2)}) collective-permute-start(f32[128,128]{1,0:T(8,128)S(1)} %shard_map.99.after), channel_id=1, source_target_pairs={{0,8},{4,12},{8,0},{12,4},{1,9},{5,13},{9,1},{13,5},{2,10},{6,14},... | collective-permute-start | bytes 196616 | tf_op jit(solution)/shard_map/ppermute | solution.py:22
  21.9 0.2 shard_map.100.after
  22.1 1.4 %collective-permute-start.6 = (f32[128,128]{1,0:T(8,128)S(1)}, f32[128,128]{1,0:T(8,128)S(1)}, u32[]{:S(2)}, u32[]{:S(2)}) collective-permute-start(f32[128,128]{1,0:T(8,128)S(1)} %shard_map.100.after), channel_id=1, source_target_pairs={{0,8},{4,12},{8,0},{12,4},{1,9},{5,13},{9,1},{13,5},{2,10},{6,14},... | collective-permute-start | bytes 196616 | tf_op jit(solution)/shard_map/ppermute | solution.py:22
  23.5 1.8 %shard_map.101 = (f32[16,128,256]{2,1,0:T(8,128)S(1)}, f32[16,128,256]{2,1,0:T(8,128)S(1)}, bf16[16,128,384]{2,1,0:T(8,128)(2,1)S(1)}, f32[8,128]{1,0:T(8,128)S(1)}) custom-call(bf16[16,128,384]{2,1,0:T(8,128)(2,1)S(1)} %get-tuple-element.21.highs_a, bf16[16,128,384]{2,1,0:T(8,128)(2,1)S(1)} %get-tuple-element.22.lows_a, ...), custom_call_target="tpu_custom_call" | custom-call | flops 1006632960 | bytes 9437184 | tf_op jit(solution)/shard_map/pallas_call | solution.py:221
  25.3 0.4 %collective-permute-done.7.received = f32[128,128]{1,0:T(8,128)S(1)} collective-permute-done((f32[128,128]{1,0:T(8,128)S(1)}, f32[128,128]{1,0:T(8,128)S(1)}, u32[]{:S(2)}, u32[]{:S(2)}) %collective-permute-start.7) | collective-permute-done | bytes 65568 | tf_op jit(solution)/shard_map/ppermute | solution.py:22
  25.8 1.3 %shard_map.103 = (f32[16,128,512]{2,1,0:T(8,128)}, f32[8,128]{1,0:T(8,128)S(1)}) custom-call(bf16[16,128,384]{2,1,0:T(8,128)(2,1)S(1)} %get-tuple-element.32.gains, f32[16,128,256]{2,1,0:T(8,128)S(1)} %get-tuple-element.34.refs_0_, f32[128,128]{1,0:T(8,128)S(1)} %shard_map.102.refs_1_.refs_6_), custom_call_target="tpu_custom_call" | custom-call | flops 201326592 | bytes 2097152 | tf_op jit(solution)/shard_map/pallas_call | solution.py:364
  27.1 0.2 collective-permute-done.6.received
  27.3 0.4 %collective-permute-start.8 = (f32[128,128]{1,0:T(8,128)S(1)}, f32[128,128]{1,0:T(8,128)S(1)}, u32[]{:S(2)}, u32[]{:S(2)}) collective-permute-start(f32[128,128]{1,0:T(8,128)S(1)} %shard_map.104.refs_3_.refs_8_), channel_id=1, source_target_pairs={{0,1},{1,0},{2,3},{3,2},{4,5},{5,4},{6,7},{7,6},{8,9},{9,8},{10,11... | collective-permute-start | bytes 196616 | tf_op jit(solution)/shard_map/ppermute | solution.py:22
  27.7 1.7 %shard_map.105 = (f32[16,128,512]{2,1,0:T(8,128)}, f32[128,128]{1,0:T(8,128)}) custom-call(bf16[16,128,384]{2,1,0:T(8,128)(2,1)S(1)} %get-tuple-element.32.gains, f32[16,128,256]{2,1,0:T(8,128)S(1)} %get-tuple-element.34.refs_0_, f32[16,128,256]{2,1,0:T(8,128)S(1)} %get-tuple-element.33.refs_1_.refs_0_, ...), custom_call_target="tpu_custom_call", output_to_operand_aliasing={{0}: (10, {})} | custom-call | flops 402653184 | bytes 4194304 | tf_op jit(solution)/shard_map/pallas_call | solution.py:364
  29.4 1.3 %shard_map.106 = f32[16,128,512]{2,1,0:T(8,128)} custom-call(bf16[16,128,384]{2,1,0:T(8,128)(2,1)S(1)} %get-tuple-element.32.gains, f32[16,128,256]{2,1,0:T(8,128)S(1)} %get-tuple-element.33.refs_1_.refs_0_, f32[128,128]{1,0:T(8,128)S(1)} %collective-permute-done.8.refs_1_, f32[16,128,512]{2,1,0:T(8,128)} %get-tuple-element.38.refs_2_), custom_call_target="tpu_custom_call", output_to_operand_aliasing={{}: (3, {})} | custom-call | flops 201326592 | bytes 2097152 | tf_op jit(solution)/shard_map/pallas_call | solution.py:364
  (18 shorter events, 0.2 us)
Async XLA Ops:
  4.6 1.5 %collective-permute-start = (f32[128,256]{1,0:T(8,128)S(1)}, f32[128,256]{1,0:T(8,128)S(1)}, u32[]{:S(2)}, u32[]{:S(2)}) collective-permute-start(f32[128,256]{1,0:T(8,128)S(1)} %get-tuple-element.29), channel_id=1, source_target_pairs={{0,1},{1,0},{2,3},{3,2},{4,5},{5,4},{6,7},{7,6},{8,9},{9,8},{10,11... | collective-permute-start | bytes 393224 | tf_op jit(solution)/shard_map/ppermute | solution.py:22
  6.1 6.8 %copy-start = (f32[1,128,512]{2,1,0:T(8,128)S(1)}, f32[1,128,512]{2,1,0:T(8,128)}, u32[]{:S(2)}) copy-start(f32[1,128,512]{2,1,0:T(8,128)} %param.13) | copy-start | bytes 786436
  6.1 6.8 %copy-start.1 = (f32[1,128,128]{2,1,0:T(8,128)S(1)}, f32[1,128,128]{2,1,0:T(8,128)}, u32[]{:S(2)}) copy-start(f32[1,128,128]{2,1,0:T(8,128)} %param.14) | copy-start | bytes 196612
  6.1 6.8 %copy-start.2 = (f32[1,128,128]{2,1,0:T(8,128)S(1)}, f32[1,128,128]{2,1,0:T(8,128)}, u32[]{:S(2)}) copy-start(f32[1,128,128]{2,1,0:T(8,128)} %param.15) | copy-start | bytes 196612
  6.1 6.8 %collective-permute-start.1 = (f32[128,256]{1,0:T(8,128)S(1)}, f32[128,256]{1,0:T(8,128)S(1)}, u32[]{:S(2)}, u32[]{:S(2)}) collective-permute-start(f32[128,256]{1,0:T(8,128)S(1)} %add.6.kept), channel_id=1, source_target_pairs={{0,2},{1,3},{2,0},{3,1},{4,6},{5,7},{6,4},{7,5},{8,10},{9,11},{10,... | collective-permute-start | bytes 393224 | tf_op jit(solution)/shard_map/ppermute | solution.py:22
  9.8 1.3 %collective-permute-start.2 = (f32[128,128]{1,0:T(8,128)S(1)}, f32[128,128]{1,0:T(8,128)S(1)}, u32[]{:S(2)}, u32[]{:S(2)}) collective-permute-start(f32[128,128]{1,0:T(8,128)S(1)} %get-tuple-element.31), channel_id=1, source_target_pairs={{0,1},{1,0},{2,3},{3,2},{4,5},{5,4},{6,7},{7,6},{8,9},{9,8},{10,11... | collective-permute-start | bytes 196616 | tf_op jit(solution)/shard_map/ppermute | solution.py:22
  11.2 4.3 %collective-permute-start.3 = (f32[128,128]{1,0:T(8,128)S(1)}, f32[128,128]{1,0:T(8,128)S(1)}, u32[]{:S(2)}, u32[]{:S(2)}) collective-permute-start(f32[128,128]{1,0:T(8,128)S(1)} %add.7.kept), channel_id=1, source_target_pairs={{0,2},{1,3},{2,0},{3,1},{4,6},{5,7},{6,4},{7,5},{8,10},{9,11},{10,... | collective-permute-start | bytes 196616 | tf_op jit(solution)/shard_map/ppermute | solution.py:22
  13.1 5.8 %collective-permute-start.4 = (f32[128,256]{1,0:T(8,128)S(1)}, f32[128,256]{1,0:T(8,128)S(1)}, u32[]{:S(2)}, u32[]{:S(2)}) collective-permute-start(f32[128,256]{1,0:T(8,128)S(1)} %shard_map.97.after), channel_id=1, source_target_pairs={{0,4},{4,0},{8,12},{12,8},{1,5},{5,1},{9,13},{13,9},{2,6},{6,2},{1... | collective-permute-start | bytes 393224 | tf_op jit(solution)/shard_map/ppermute | solution.py:22
  15.7 6.2 %collective-permute-start.5 = (f32[128,128]{1,0:T(8,128)S(1)}, f32[128,128]{1,0:T(8,128)S(1)}, u32[]{:S(2)}, u32[]{:S(2)}) collective-permute-start(f32[128,128]{1,0:T(8,128)S(1)} %shard_map.98.after.mine.refs_7_), channel_id=1, source_target_pairs={{0,4},{4,0},{8,12},{12,8},{1,5},{5,1},{9,13},{13,9},{2,6},{6,2},{1... | collective-permute-start | bytes 196616 | tf_op jit(solution)/shard_map/ppermute | solution.py:22
  19.1 6.6 %collective-permute-start.7 = (f32[128,128]{1,0:T(8,128)S(1)}, f32[128,128]{1,0:T(8,128)S(1)}, u32[]{:S(2)}, u32[]{:S(2)}) collective-permute-start(f32[128,128]{1,0:T(8,128)S(1)} %shard_map.99.after), channel_id=1, source_target_pairs={{0,8},{4,12},{8,0},{12,4},{1,9},{5,13},{9,1},{13,5},{2,10},{6,14},... | collective-permute-start | bytes 196616 | tf_op jit(solution)/shard_map/ppermute | solution.py:22
  22.1 5.2 %collective-permute-start.6 = (f32[128,128]{1,0:T(8,128)S(1)}, f32[128,128]{1,0:T(8,128)S(1)}, u32[]{:S(2)}, u32[]{:S(2)}) collective-permute-start(f32[128,128]{1,0:T(8,128)S(1)} %shard_map.100.after), channel_id=1, source_target_pairs={{0,8},{4,12},{8,0},{12,4},{1,9},{5,13},{9,1},{13,5},{2,10},{6,14},... | collective-permute-start | bytes 196616 | tf_op jit(solution)/shard_map/ppermute | solution.py:22
  25.7 1.9 %collective-permute-start.9 = (f32[128,128]{1,0:T(8,128)S(1)}, f32[128,128]{1,0:T(8,128)S(1)}, u32[]{:S(2)}, u32[]{:S(2)}) collective-permute-start(f32[128,128]{1,0:T(8,128)S(1)} %shard_map.102.refs_1_.refs_6_), channel_id=1, source_target_pairs={{0,1},{1,0},{2,3},{3,2},{4,5},{5,4},{6,7},{7,6},{8,9},{9,8},{10,11... | collective-permute-start | bytes 196616 | tf_op jit(solution)/shard_map/ppermute | solution.py:22
  27.3 2.1 %collective-permute-start.8 = (f32[128,128]{1,0:T(8,128)S(1)}, f32[128,128]{1,0:T(8,128)S(1)}, u32[]{:S(2)}, u32[]{:S(2)}) collective-permute-start(f32[128,128]{1,0:T(8,128)S(1)} %shard_map.104.refs_3_.refs_8_), channel_id=1, source_target_pairs={{0,1},{1,0},{2,3},{3,2},{4,5},{5,4},{6,7},{7,6},{8,9},{9,8},{10,11... | collective-permute-start | bytes 196616 | tf_op jit(solution)/shard_map/ppermute | solution.py:22
